TPU v7x, 32 devices: a whole 2x2x4 slice. The times are simulated.
32 devices in a mesh: blk: 16 (over z, y, core), tp: 2 (over x).
Axes of the slice: x: 2, y: 2, z: 4, core: 2. Of those that a mesh axis runs over, the one named last changes fastest.
Arguments:
- frames: bfloat16 [4096, 1024], P('blk'), may hold values from -6 to 6
- clip_lengths: int32 [8], replicated, may hold values from 1 to 3841, 4096 in all
- text_states: bfloat16 [128, 1024], replicated, may hold values from -6 to 6
- text_segments: int32 [128], replicated, may hold values from 0 to 7, never falling along the last dimension, each value on 1 to 32 neighbouring positions
- gain_one: float32 [1024], replicated, may hold values from 0.1 to 1.9
- shift_one: float32 [1024], replicated, may hold values from -1.5 to 1.5
- gain_two: float32 [1024], replicated, may hold values from 0.1 to 1.9
- shift_two: float32 [1024], replicated, may hold values from -1.5 to 1.5
- gain_three: float32 [1024], replicated, may hold values from 0.1 to 1.9
- shift_three: float32 [1024], replicated, may hold values from -1.5 to 1.5
- query_weight: bfloat16 [1024, 1024], P(None, 'tp'), may hold values from -0.1875 to 0.1875
- key_weight: bfloat16 [1024, 1024], P(None, 'tp'), may hold values from -0.1875 to 0.1875
- value_weight: bfloat16 [1024, 1024], P(None, 'tp'), may hold values from -0.1875 to 0.1875
- output_weight: bfloat16 [1024, 1024], P('tp'), may hold values from -0.75 to 0.75
- cross_query: bfloat16 [1024, 1024], P(None, 'tp'), may hold values from -0.1875 to 0.1875
- cross_key: bfloat16 [1024, 1024], P(None, 'tp'), may hold values from -0.1875 to 0.1875
- cross_value: bfloat16 [1024, 1024], P(None, 'tp'), may hold values from -0.1875 to 0.1875
- cross_output: bfloat16 [1024, 1024], P('tp'), may hold values from -0.375 to 0.375
- inner_weight: bfloat16 [1024, 4096], P(None, 'tp'), may hold values from -0.1875 to 0.1875
- outer_weight: bfloat16 [4096, 1024], P('tp'), may hold values from -0.09375 to 0.09375
- cotangent: bfloat16 [4096, 1024], P('blk'), may hold values from -6 to 6
Outputs:
- result: bfloat16 [4096, 1024], P('blk')
- grad_frames: bfloat16 [4096, 1024], P('blk')
- grad_text: float32 [128, 1024], replicated
- grad_gain_one: float32 [1024], replicated
- grad_shift_one: float32 [1024], replicated
- grad_gain_two: float32 [1024], replicated
- grad_shift_two: float32 [1024], replicated
- grad_gain_three: float32 [1024], replicated
- grad_shift_three: float32 [1024], replicated
- grad_query_weight: float32 [1024, 1024], P(None, 'tp')
- grad_key_weight: float32 [1024, 1024], P(None, 'tp')
- grad_value_weight: float32 [1024, 1024], P(None, 'tp')
- grad_output_weight: float32 [1024, 1024], P('tp')
- grad_cross_query: float32 [1024, 1024], P(None, 'tp')
- grad_cross_key: float32 [1024, 1024], P(None, 'tp')
- grad_cross_value: float32 [1024, 1024], P(None, 'tp')
- grad_cross_output: float32 [1024, 1024], P('tp')
- grad_inner_weight: float32 [1024, 4096], P(None, 'tp')
- grad_outer_weight: float32 [4096, 1024], P('tp')
Inputs may be any that keep to these rules, and one draw needn't show every extreme that they name: `clip_lengths`: clips follow one another in the pack; one of them has 3841 frames. `text_segments`: text tokens of a clip stand together and in clip order; every clip has 1 to 32 of them, one exactly 32.
All inputs are finite; a program needn't handle non-finite values.
Results may differ from a plain program's by a relative error of at most 0.028.
Values may be sent and summed in bfloat16 or wider, within the bound.
No kernel may reach another device: no remote copies, remote signals or barrier semaphores. Data moves between devices by JAX's collectives and lax.ppermute only.
A program may use at most 384 MiB of HBM per device.

v0:
```python
import jax
import jax.numpy as jnp
from jax import lax
from jax.sharding import PartitionSpec as P

HEAD_DIM = 64


EPSILON = 1e-05
NEGATIVE = -1e30


def shifted(block, axis, distance):
    devices = range(lax.axis_size(axis))
    route = [(i - distance, i) for i in devices if i - distance in devices]
    return lax.ppermute(block, axis, route)


def shifted_2(value, axis, by):
    size = lax.axis_size(axis)
    return lax.ppermute(value, axis, [(i, (i + by) % size) for i in range(size)])


def layer_norm(values, gain, shift):
    centre = values - jnp.mean(values, axis=-1, keepdims=True)
    spread = jnp.mean(centre * centre, axis=-1, keepdims=True)
    return centre * lax.rsqrt(spread + EPSILON) * gain + shift


def norm_grads(values, gain, shift, grad):
    _, pullback = jax.vjp(layer_norm, values, gain, shift)
    return pullback(grad)


def gelu_exact(values):
    return jax.nn.gelu(values, approximate=False)


def clip_rows(positions, clip_lengths):
    ends = jnp.cumsum(clip_lengths)
    starts = ends - clip_lengths
    segment = jnp.sum((positions[:, None] >= ends[None, :]).astype(jnp.int32), axis=1)
    match = segment[:, None] == jnp.arange(clip_lengths.shape[0], dtype=jnp.int32)[None, :]
    first = jnp.sum(jnp.where(match, starts[None, :], 0), axis=1)
    return (segment, first)


def matmul(left, right):
    return jnp.dot(left, right, preferred_element_type=jnp.float32)


def head_sum(values):
    return lax.psum(values.astype(jnp.bfloat16), "tp").astype(jnp.float32)


def unchanged(state):
    return state


def block_grads(
    query_heads,
    grad_heads,
    log_total,
    delta,
    query_rows,
    query_first,
    key_heads,
    value_heads,
    key_rows,
):
    allowed = (key_rows[None, :] <= query_rows[:, None]) & (
        key_rows[None, :] >= query_first[:, None]
    )
    score = jnp.einsum("qhd,khd->hqk", query_heads, key_heads, preferred_element_type=jnp.float32)
    weights = jnp.exp(jnp.where(allowed[None], score - log_total[:, :, None], NEGATIVE))
    grad_weights = jnp.einsum(
        "qhd,khd->hqk", grad_heads, value_heads, preferred_element_type=jnp.float32
    )
    grad_score = (weights * (grad_weights - delta[:, :, None])).astype(jnp.bfloat16)
    query_part = jnp.einsum(
        "hqk,khd->qhd", grad_score, key_heads, preferred_element_type=jnp.float32
    )
    key_part = jnp.einsum(
        "hqk,qhd->khd", grad_score, query_heads, preferred_element_type=jnp.float32
    )
    value_part = jnp.einsum(
        "hqk,qhd->khd", weights.astype(jnp.bfloat16), grad_heads, preferred_element_type=jnp.float32
    )
    return (query_part, key_part, value_part)


def shards(
    frames,
    clip_lengths,
    text_states,
    text_segments,
    gain_one,
    shift_one,
    gain_two,
    shift_two,
    gain_three,
    shift_three,
    query_weight,
    key_weight,
    value_weight,
    output_weight,
    cross_query,
    cross_key,
    cross_value,
    cross_output,
    inner_weight,
    outer_weight,
    cotangent,
):
    row_count = frames.shape[0]
    text_count = text_states.shape[0]
    width_here = query_weight.shape[1]
    heads_here = width_here // HEAD_DIM
    blk_count = lax.axis_size("blk")
    blk_index = lax.axis_index("blk")
    scale = float(HEAD_DIM) ** (-0.5)
    my_first_row = blk_index * row_count
    offsets = jnp.arange(row_count, dtype=jnp.int32)
    rows = my_first_row + offsets
    segment, first = clip_rows(rows, clip_lengths)
    inputs = frames.astype(jnp.float32)
    normed_one = layer_norm(inputs, gain_one, shift_one).astype(jnp.bfloat16)
    queries = (matmul(normed_one, query_weight) * scale).astype(jnp.bfloat16)
    keys = matmul(normed_one, key_weight).astype(jnp.bfloat16)
    values = matmul(normed_one, value_weight).astype(jnp.bfloat16)
    query_heads = queries.reshape(row_count, heads_here, HEAD_DIM)
    start_state = (
        jnp.zeros((row_count, heads_here, HEAD_DIM), jnp.float32),
        jnp.full((heads_here, row_count), NEGATIVE, jnp.float32),
        jnp.zeros((heads_here, row_count), jnp.float32),
    )
    start = jnp.int32(0)
    key_piece = lax.all_gather(keys, "blk", axis=0, tiled=True)
    value_piece = lax.all_gather(values, "blk", axis=0, tiled=True)
    count = key_piece.shape[0]
    key_rows = jnp.arange(count, dtype=jnp.int32)

    def fold_work(state):
        totals, run_max, run_sum = state
        piece_keys = key_piece.reshape(count, heads_here, HEAD_DIM)
        piece_values = value_piece.reshape(count, heads_here, HEAD_DIM)
        score = jnp.einsum(
            "qhd,khd->hqk", query_heads, piece_keys, preferred_element_type=jnp.float32
        )
        allowed = (key_rows[None, :] <= rows[:, None]) & (key_rows[None, :] >= first[:, None])
        masked = jnp.where(allowed[None], score, NEGATIVE)
        new_max = jnp.maximum(run_max, jnp.max(masked, axis=-1))
        expo = jnp.where(allowed[None], jnp.exp(masked - new_max[:, :, None]), 0.0)
        run_sum = jnp.sum(expo, axis=-1)
        added = jnp.einsum(
            "hqk,khd->qhd",
            expo.astype(jnp.bfloat16),
            piece_values,
            preferred_element_type=jnp.float32,
        )
        totals = added
        return (totals, new_max, run_sum)

    needed = (start <= rows[-1]) & (start + count - 1 >= first[0])
    totals, run_max, run_sum = lax.cond(needed, fold_work, unchanged, start_state)
    self_out = totals / jnp.transpose(run_sum)[:, :, None]
    log_total = run_max + jnp.log(run_sum)
    attended = self_out.reshape(row_count, width_here).astype(jnp.bfloat16)
    first_sum = inputs + head_sum(matmul(attended, output_weight))
    normed_two = layer_norm(first_sum, gain_two, shift_two).astype(jnp.bfloat16)
    cross_queries = (matmul(normed_two, cross_query) * scale).astype(jnp.bfloat16)
    text_keys = matmul(text_states, cross_key).astype(jnp.bfloat16)
    text_values = matmul(text_states, cross_value).astype(jnp.bfloat16)
    cross_heads = cross_queries.reshape(row_count, heads_here, HEAD_DIM)
    text_key_heads = text_keys.reshape(text_count, heads_here, HEAD_DIM)
    text_value_heads = text_values.reshape(text_count, heads_here, HEAD_DIM)
    allowed_text = segment[:, None] == text_segments[None, :]
    cross_score = jnp.einsum(
        "qhd,khd->hqk", cross_heads, text_key_heads, preferred_element_type=jnp.float32
    )
    cross_masked = jnp.where(allowed_text[None], cross_score, NEGATIVE)
    cross_max = jnp.max(cross_masked, axis=-1, keepdims=True)
    cross_expo = jnp.where(allowed_text[None], jnp.exp(cross_masked - cross_max), 0.0)
    cross_weights = cross_expo / jnp.sum(cross_expo, axis=-1, keepdims=True)
    cross_weights_low = cross_weights.astype(jnp.bfloat16)
    cross_out = jnp.einsum(
        "hqk,khd->qhd", cross_weights_low, text_value_heads, preferred_element_type=jnp.float32
    )
    crossed = cross_out.reshape(row_count, width_here).astype(jnp.bfloat16)
    second_sum = first_sum + head_sum(matmul(crossed, cross_output))
    normed_three = layer_norm(second_sum, gain_three, shift_three).astype(jnp.bfloat16)
    hidden_pre = matmul(normed_three, inner_weight)
    hidden = gelu_exact(hidden_pre).astype(jnp.bfloat16)
    output = second_sum + head_sum(matmul(hidden, outer_weight))
    grad_output = cotangent.astype(jnp.float32)
    grad_outer = matmul(hidden.T, cotangent)
    grad_hidden = matmul(cotangent, outer_weight.T)
    _, gelu_back = jax.vjp(gelu_exact, hidden_pre)
    grad_pre = gelu_back(grad_hidden)[0].astype(jnp.bfloat16)
    grad_inner = matmul(normed_three.T, grad_pre)
    grad_normed_three = head_sum(matmul(grad_pre, inner_weight.T))
    through_three, grad_gain_three, grad_shift_three = norm_grads(
        second_sum, gain_three, shift_three, grad_normed_three
    )
    grad_second = grad_output + through_three
    grad_second_low = grad_second.astype(jnp.bfloat16)
    grad_cross_output = matmul(crossed.T, grad_second_low)
    grad_crossed = (
        matmul(grad_second_low, cross_output.T)
        .astype(jnp.bfloat16)
        .reshape(row_count, heads_here, HEAD_DIM)
    )
    grad_cross_weights = jnp.einsum(
        "qhd,khd->hqk", grad_crossed, text_value_heads, preferred_element_type=jnp.float32
    )
    cross_delta = jnp.transpose(jnp.sum(grad_crossed.astype(jnp.float32) * cross_out, axis=-1))
    grad_cross_score = (cross_weights * (grad_cross_weights - cross_delta[:, :, None])).astype(
        jnp.bfloat16
    )
    grad_cross_heads = jnp.einsum(
        "hqk,khd->qhd", grad_cross_score, text_key_heads, preferred_element_type=jnp.float32
    ).astype(jnp.bfloat16)
    grad_cross_queries = (grad_cross_heads * scale).reshape(row_count, width_here)
    text_key_part = jnp.einsum(
        "hqk,qhd->khd", grad_cross_score, cross_heads, preferred_element_type=jnp.float32
    )
    text_value_part = jnp.einsum(
        "hqk,qhd->khd", cross_weights_low, grad_crossed, preferred_element_type=jnp.float32
    )
    grad_text_keys, grad_text_values = lax.psum(
        (
            text_key_part.reshape(text_count, width_here),
            text_value_part.reshape(text_count, width_here),
        ),
        "blk",
    )
    grad_text_keys = grad_text_keys.astype(jnp.bfloat16)
    grad_text_values = grad_text_values.astype(jnp.bfloat16)
    grad_cross_key = matmul(text_states.T, grad_text_keys)
    grad_cross_value = matmul(text_states.T, grad_text_values)
    grad_text = lax.psum(
        (matmul(grad_text_keys, cross_key.T) + matmul(grad_text_values, cross_value.T)).astype(
            jnp.bfloat16
        ),
        "tp",
    ).astype(jnp.float32)
    grad_cross_query = matmul(normed_two.T, grad_cross_queries)
    grad_normed_two = head_sum(matmul(grad_cross_queries, cross_query.T))
    through_two, grad_gain_two, grad_shift_two = norm_grads(
        first_sum, gain_two, shift_two, grad_normed_two
    )
    grad_first = grad_second + through_two
    grad_first_low = grad_first.astype(jnp.bfloat16)
    grad_output_weight = matmul(attended.T, grad_first_low)
    grad_attended = matmul(grad_first_low, output_weight.T).astype(jnp.bfloat16)
    grad_heads = grad_attended.reshape(row_count, heads_here, HEAD_DIM)
    self_delta = jnp.transpose(jnp.sum(grad_heads.astype(jnp.float32) * self_out, axis=-1))
    zero_block = jnp.zeros((row_count, width_here), jnp.float32)

    def key_turn(turn, carry):
        source = (blk_index - turn) % blk_count
        base = source * row_count

        def key_work(state):
            key_block, value_block, key_grad, value_grad, query_grad = state
            query_part, key_part, value_part = block_grads(
                query_heads,
                grad_heads,
                log_total,
                self_delta,
                rows,
                first,
                key_block.reshape(row_count, heads_here, HEAD_DIM),
                value_block.reshape(row_count, heads_here, HEAD_DIM),
                base + offsets,
            )
            return (
                key_block,
                value_block,
                key_grad + key_part.reshape(row_count, width_here),
                value_grad + value_part.reshape(row_count, width_here),
                query_grad + query_part.reshape(row_count, width_here),
            )

        needed = (base <= rows[-1]) & (base + row_count - 1 >= first[0])
        key_block, value_block, key_grad, value_grad, query_grad = lax.cond(
            needed, key_work, unchanged, carry
        )
        key_block, value_block = shifted((key_block, value_block), "blk", 1)
        key_grad, value_grad = (
            shifted_2(key_grad.astype(jnp.bfloat16), "blk", 1).astype(key_grad.dtype),
            shifted_2(value_grad.astype(jnp.bfloat16), "blk", 1).astype(value_grad.dtype),
        )
        return (key_block, value_block, key_grad, value_grad, query_grad)

    final = lax.fori_loop(
        0, blk_count, key_turn, (keys, values, zero_block, zero_block, zero_block)
    )
    key_total, value_total, query_total = (final[2], final[3], final[4])
    grad_queries = query_total.astype(jnp.bfloat16) * scale
    grad_keys = key_total.astype(jnp.bfloat16)
    grad_values = value_total.astype(jnp.bfloat16)
    grad_query_weight = matmul(normed_one.T, grad_queries)
    grad_key_weight = matmul(normed_one.T, grad_keys)
    grad_value_weight = matmul(normed_one.T, grad_values)
    grad_normed_one = head_sum(
        matmul(grad_queries, query_weight.T)
        + matmul(grad_keys, key_weight.T)
        + matmul(grad_values, value_weight.T)
    )
    through_one, grad_gain_one, grad_shift_one = norm_grads(
        inputs, gain_one, shift_one, grad_normed_one
    )
    grad_frames = (grad_first + through_one).astype(jnp.bfloat16)
    (
        grad_query_weight,
        grad_key_weight,
        grad_value_weight,
        grad_output_weight,
        grad_cross_query,
        grad_cross_output,
        grad_inner,
        grad_outer,
        grad_gain_one,
        grad_shift_one,
        grad_gain_two,
        grad_shift_two,
        grad_gain_three,
        grad_shift_three,
    ) = lax.psum(
        (
            grad_query_weight,
            grad_key_weight,
            grad_value_weight,
            grad_output_weight,
            grad_cross_query,
            grad_cross_output,
            grad_inner,
            grad_outer,
            grad_gain_one,
            grad_shift_one,
            grad_gain_two,
            grad_shift_two,
            grad_gain_three,
            grad_shift_three,
        ),
        "blk",
    )
    return (
        output.astype(jnp.bfloat16),
        grad_frames,
        grad_text,
        grad_gain_one,
        grad_shift_one,
        grad_gain_two,
        grad_shift_two,
        grad_gain_three,
        grad_shift_three,
        grad_query_weight,
        grad_key_weight,
        grad_value_weight,
        grad_output_weight,
        grad_cross_query,
        grad_cross_key,
        grad_cross_value,
        grad_cross_output,
        grad_inner,
        grad_outer,
    )


def solution(mesh):
    return jax.shard_map(
        shards,
        mesh=mesh,
        in_specs=(
            P("blk", None),
            P(),
            P(),
            P(),
            P(),
            P(),
            P(),
            P(),
            P(),
            P(),
            P(None, "tp"),
            P(None, "tp"),
            P(None, "tp"),
            P("tp", None),
            P(None, "tp"),
            P(None, "tp"),
            P(None, "tp"),
            P("tp", None),
            P(None, "tp"),
            P("tp", None),
            P("blk", None),
        ),
        out_specs=(
            P("blk", None),
            P("blk", None),
            P(),
            P(),
            P(),
            P(),
            P(),
            P(),
            P(),
            P(None, "tp"),
            P(None, "tp"),
            P(None, "tp"),
            P("tp", None),
            P(None, "tp"),
            P(None, "tp"),
            P(None, "tp"),
            P("tp", None),
            P(None, "tp"),
            P("tp", None),
        ),
        check_vma=False,
    )
```

profile of v0, /device:TPU:0, one launch (start us, length us, event | category | flops | bytes accessed | tf_op | source)
XLA Modules:
  0.0 1469.3 jit_solution(12834105977165518617)
XLA Ops:
  10.0 2.6 convolution_convert_fusion.9
  21.8 44.4 %all-gather.3.cloned.1.call-done = bf16[4096,512]{1,0:T(8,128)(2,1)} async-done(((bf16[256,512]{1,0:T(8,128)(2,1)}), bf16[4096,512]{1,0:T(8,128)(2,1)}) %all-gather.3.cloned.1.call-update) | async-done | bytes 4194320 | tf_op jit(solution)/shard_map/all_gather | solution.py:138
  66.2 51.8 %all-gather.5.cloned.1.call-done = bf16[4096,512]{1,0:T(8,128)(2,1)} async-done(((bf16[256,512]{1,0:T(8,128)(2,1)}), bf16[4096,512]{1,0:T(8,128)(2,1)}) %all-gather.5.cloned.1.call-update) | async-done | bytes 4194320 | tf_op jit(solution)/shard_map/all_gather | solution.py:139
  118.1 62.9 %conditional.2 = (f32[256,8,64]{0,2,1:T(8,128)S(1)}, f32[8,256]{1,0:T(8,128)}, f32[8,256]{1,0:T(8,128)}, f32[8,256]{1,0:T(8,128)S(1)}) conditional(s32[]{:T(128)} %bitcast.13, () %tuple.55, (s32[4096]{0:T(1024)S(1)}, s32[4096]{0:T(1024)S(1)}, s32[256]{0:T(256)}, s32[256]{0:T(256)}, bf16[4096,512]{1,0:T(8,128)(2,1)}, ...), branch_computations={%region_5.6_spmd, %region_6.9_spmd} | conditional | flops 2234513408 | bytes 130910240 | solution.py:165
  118.1 6.3 copy.81
  126.0 6.3 copy.80
  132.3 15.7 %select_reduce_fusion = (f32[8,256]{1,0:T(8,128)S(1)}, f32[8,256,4096]{2,1,0:T(8,128)}) fusion(pred[256,4096]{1,0:T(8,128)(4,1)S(1)} %compare_and_fusion, bf16[256,8,64]{0,2,1:T(8,128)(2,1)S(1)} %get-tuple-element.475, bf16[4096,8,64]{0,2,1:T(8,128)(2,1)} %bitcast.126), kind=kOutput, calls=%fused_computation.2 | convolution fusion | flops 1090516992 | bytes 39067648 | tf_op jit(solution)/shard_map/cond/branch_1_fun/qhd,khd->hqk/dot_general | solution.py:147
  148.6 15.5 %fusion.7 = f32[256,8,64]{0,2,1:T(8,128)S(1)} fusion(bf16[4096,8,64]{0,2,1:T(8,128)(2,1)} %bitcast.133, f32[8,256,4096]{2,1,0:T(8,128)} %get-tuple-element.768, f32[8,256]{1,0:T(8,128)} %broadcast_maximum_fusion, pred[256,4096]{1,0:T(8,128)(4,1)S(1)} %compare_and_fusion), kind=kOutput, calls=%fused_computation.8 | convolution fusion | flops 1107296256 | bytes 39329792 | tf_op jit(solution)/shard_map/cond/branch_1_fun/hqk,khd->qhd/dot_general | solution.py:155
  164.1 16.2 %fusion.2 = f32[8,256]{1,0:T(8,128)} fusion(f32[8,256,4096]{2,1,0:T(8,128)} %get-tuple-element.768, f32[8,256]{1,0:T(8,128)} %broadcast_maximum_fusion, pred[256,4096]{1,0:T(8,128)(4,1)S(1)} %compare_and_fusion), kind=kLoop, calls=%fused_computation.3 | loop fusion | flops 33552384 | bytes 34619392 | tf_op jit(solution)/shard_map/cond/branch_1_fun/reduce_sum | solution.py:154
  181.8 2.6 convolution_convert_fusion.2
  189.4 22.3 %all-reduce.12.cloned.1.call-done = bf16[256,1024]{1,0:T(8,128)(2,1)} async-done(((bf16[256,1024]{1,0:T(8,128)(2,1)}), bf16[256,1024]{1,0:T(8,128)(2,1)}) %all-reduce.12.cloned.1.call-update) | async-done | bytes 524304 | tf_op jit(solution)/shard_map/psum | solution.py:53
  228.5 25.3 %all-reduce.14.cloned.1.call-done = bf16[256,1024]{1,0:T(8,128)(2,1)} async-done(((bf16[256,1024]{1,0:T(8,128)(2,1)}), bf16[256,1024]{1,0:T(8,128)(2,1)}) %all-reduce.14.cloned.1.call-update) | async-done | bytes 524304 | tf_op jit(solution)/shard_map/psum | solution.py:53
  256.6 3.7 fusion.86
  260.3 6.6 add_convert_fusion
  272.1 6.2 fusion.105
  280.4 4.8 fusion.85
  285.3 15.5 %all-reduce.16.cloned.1.call-done = bf16[256,1024]{1,0:T(8,128)(2,1)} async-done(((bf16[256,1024]{1,0:T(8,128)(2,1)}), bf16[256,1024]{1,0:T(8,128)(2,1)}) %all-reduce.16.cloned.1.call-update) | async-done | bytes 524304 | tf_op jit(solution)/shard_map/psum | solution.py:53
  317.9 25.5 %all-reduce.18.cloned.1.call-done = bf16[256,1024]{1,0:T(8,128)(2,1)} async-done(((bf16[256,1024]{1,0:T(8,128)(2,1)}), bf16[256,1024]{1,0:T(8,128)(2,1)}) %all-reduce.18.cloned.1.call-update) | async-done | bytes 524304 | tf_op jit(solution)/shard_map/psum | solution.py:53
  353.5 421.7 %while.26 = (s32[]{:T(128)}, bf16[256,512]{0,1:T(8,128)(2,1)S(1)}, bf16[256,512]{0,1:T(8,128)(2,1)}, f32[256,512]{0,1:T(8,128)}, f32[256,512]{0,1:T(8,128)}, /*i...) while((s32[]{:T(128)}, bf16[256,512]{0,1:T(8,128)(2,1)S(1)}, ...), condition=%wide.region_29.30_spmd.clone, body=%wide.region_26.29_spmd.clone.sunk | while | flops 341115168 | bytes 37714808 | solution.py:296
  359.3 5.0 conditional.5
  368.6 3.5 collective-permute-start.1
  384.3 6.3 collective-permute-start.2
  395.7 4.4 collective-permute-start.1
  413.4 7.3 collective-permute-start.3
  422.8 5.2 collective-permute-start.1
  443.2 7.5 collective-permute-start
  450.7 5.2 collective-permute-start.1
  473.6 10.1 collective-permute-start.1
  501.5 5.2 collective-permute-start.1
  517.2 2.9 collective-permute-start.2
  525.7 5.2 collective-permute-start.1
  543.8 6.3 collective-permute-start.3
  550.0 3.6 collective-permute-start
  553.6 5.2 collective-permute-start.1
  574.1 7.4 collective-permute-start
  581.5 5.2 collective-permute-start.1
  601.9 2.6 collective-permute-start
  604.5 9.1 collective-permute-start.1
  624.0 2.7 collective-permute-start.2
  629.8 2.6 collective-permute-start
  632.4 5.2 collective-permute-start.1
  648.0 2.8 collective-permute-start.2
  654.0 2.6 collective-permute-start
  656.6 5.2 collective-permute-start.1
  674.6 5.3 collective-permute-start.3
  679.9 4.6 collective-permute-start
  684.5 5.2 collective-permute-start.1
  704.9 7.4 collective-permute-start
  712.3 5.2 collective-permute-start.1
  732.7 2.6 collective-permute-start
  735.3 8.1 collective-permute-start.1
  754.3 3.2 collective-permute-start.2
  760.7 2.6 collective-permute-start
  763.2 5.2 collective-permute-start.1
  779.9 2.9 fusion.104
  784.8 31.8 %all-reduce.20.cloned.1.call-done = bf16[256,1024]{1,0:T(8,128)(2,1)} async-done(((bf16[256,1024]{1,0:T(8,128)(2,1)}), bf16[256,1024]{1,0:T(8,128)(2,1)}) %all-reduce.20.cloned.1.call-update) | async-done | bytes 524304 | tf_op jit(solution)/shard_map/psum | solution.py:53
  820.3 67.9 %all-reduce.25 = (bf16[128,512]{0,1:T(8,128)(2,1)S(1)}, bf16[128,512]{0,1:T(8,128)(2,1)}, f32[1024]{0:T(1024)}, f32[1024]{0:T(1024)}, f32[1024]{0:T(1024)}, /*in...) all-reduce(f32[128,512]{0,1:T(8,128)S(1)} %bitcast.142, ...), channel_id=1, replica_groups=mesh['blk'=16,'tp'=2] {'blk'}, use_global_device_ids=true, to_apply=%region_33.34 | all-reduce | flops 137216 | bytes 835584 | tf_op jit(solution)/shard_map/psum | solution.py:230
  900.7 2.9 copy.94
  905.4 2.9 copy.95
  909.5 13.5 all-reduce.24.cloned.1.call-done
  926.8 512.8 %all-reduce.22.cloned.1.call-done = (f32[1024,512]{1,0:T(8,128)}, f32[1024,512]{1,0:T(8,128)}, f32[1024,512]{1,0:T(8,128)}, f32[512,1024]{1,0:T(8,128)}, f32[102...) async-done(((f32[1024,512]{1,0:T(8,128)}, f32[1024,512]{1,0:T(8,128)}, f32[1024,512]{1,0:T(8,128)}, f32[512,1024]{1,0:T(8,128)}, ...) | async-done | bytes 29360144 | tf_op jit(solution)/shard_map/psum | solution.py:330
  1439.6 3.2 copy.158
  1453.2 4.3 copy.164
  1458.9 3.4 copy.165
  (680 shorter events, 340.4 us)
Async XLA Ops:
  7.3 59.0 %all-gather.3.cloned.1.call-start = ((), (), s32[]{:S(2)}) async-start(), calls=%async_computation | async-start | bytes 4456448 | tf_op jit(solution)/shard_map/all_gather | solution.py:138
  12.7 105.4 %all-gather.5.cloned.1.call-start = ((), (), s32[]{:S(2)}) async-start(), calls=%async_computation.1 | async-start | bytes 4456448 | tf_op jit(solution)/shard_map/all_gather | solution.py:139
  14.0 197.7 %all-reduce.12.cloned.1.call-start = ((), (), s32[]{:S(2)}) async-start(), calls=%async_computation.2 | async-start | bytes 1048576 | tf_op jit(solution)/shard_map/psum | solution.py:53
  184.4 69.4 %all-reduce.14.cloned.1.call-start = ((), (), s32[]{:S(2)}) async-start(), calls=%async_computation.3 | async-start | bytes 1048576 | tf_op jit(solution)/shard_map/psum | solution.py:53
  225.1 75.7 %all-reduce.16.cloned.1.call-start = ((), (), s32[]{:S(2)}) async-start(), calls=%async_computation.4 | async-start | bytes 1048576 | tf_op jit(solution)/shard_map/psum | solution.py:53
  272.0 71.5 %all-reduce.18.cloned.1.call-start = ((), (), s32[]{:S(2)}) async-start(), calls=%async_computation.5 | async-start | bytes 1048576 | tf_op jit(solution)/shard_map/psum | solution.py:53
  314.7 501.9 %all-reduce.20.cloned.1.call-start = ((), (), s32[]{:S(2)}) async-start(), calls=%async_computation.6 | async-start | bytes 1048576 | tf_op jit(solution)/shard_map/psum | solution.py:53
  364.3 8.7 collective-permute-start.2
  365.1 10.6 collective-permute-start.3
  366.7 9.8 collective-permute-start
  368.6 7.9 collective-permute-start.1
  384.3 15.7 %collective-permute-start.2 = (bf16[256,512]{0,1:T(8,128)(2,1)S(1)}, bf16[256,512]{0,1:T(8,128)(2,1)}, u32[]{:S(2)}, u32[]{:S(2)}) collective-permute-start(bf16[256,512]{0,1:T(8,128)(2,1)S(1)} %convert_element_type.500), channel_id=1, source_target_pairs={{0,2},{2,4},{4,6},{6,8},{8,10},{10,12},{12,14},{14,16},{16,18},{18... | collective-permute-start | bytes 786440 | tf_op jit(solution)/shard_map/while/body/eval_jaxpr/ppermute | solution.py:21
  391.3 10.5 collective-permute-start.3
  393.7 8.9 collective-permute-start
  410.5 17.5 %collective-permute-start.2 = (bf16[256,512]{0,1:T(8,128)(2,1)S(1)}, bf16[256,512]{0,1:T(8,128)(2,1)}, u32[]{:S(2)}, u32[]{:S(2)}) collective-permute-start(bf16[256,512]{0,1:T(8,128)(2,1)S(1)} %convert_element_type.500), channel_id=1, source_target_pairs={{0,2},{2,4},{4,6},{6,8},{8,10},{10,12},{12,14},{14,16},{16,18},{18... | collective-permute-start | bytes 786440 | tf_op jit(solution)/shard_map/while/body/eval_jaxpr/ppermute | solution.py:21
  413.4 16.3 %collective-permute-start.3 = (bf16[256,512]{0,1:T(8,128)(2,1)}, bf16[256,512]{0,1:T(8,128)(2,1)S(1)}, u32[]{:S(2)}, u32[]{:S(2)}) collective-permute-start(bf16[256,512]{0,1:T(8,128)(2,1)} %convert_element_type.502), channel_id=1, source_target_pairs={{0,2},{2,4},{4,6},{6,8},{8,10},{10,12},{12,14},{14,16},{16,18},{18... | collective-permute-start | bytes 786440 | tf_op jit(solution)/shard_map/while/body/eval_jaxpr/ppermute | solution.py:21
  420.7 9.8 collective-permute-start
  422.8 7.8 collective-permute-start.1
  438.4 17.5 %collective-permute-start.2 = (bf16[256,512]{0,1:T(8,128)(2,1)S(1)}, bf16[256,512]{0,1:T(8,128)(2,1)}, u32[]{:S(2)}, u32[]{:S(2)}) collective-permute-start(bf16[256,512]{0,1:T(8,128)(2,1)S(1)} %convert_element_type.500), channel_id=1, source_target_pairs={{0,2},{2,4},{4,6},{6,8},{8,10},{10,12},{12,14},{14,16},{16,18},{18... | collective-permute-start | bytes 786440 | tf_op jit(solution)/shard_map/while/body/eval_jaxpr/ppermute | solution.py:21
  440.8 16.8 %collective-permute-start.3 = (bf16[256,512]{0,1:T(8,128)(2,1)}, bf16[256,512]{0,1:T(8,128)(2,1)S(1)}, u32[]{:S(2)}, u32[]{:S(2)}) collective-permute-start(bf16[256,512]{0,1:T(8,128)(2,1)} %convert_element_type.502), channel_id=1, source_target_pairs={{0,2},{2,4},{4,6},{6,8},{8,10},{10,12},{12,14},{14,16},{16,18},{18... | collective-permute-start | bytes 786440 | tf_op jit(solution)/shard_map/while/body/eval_jaxpr/ppermute | solution.py:21
  443.2 15.3 %collective-permute-start = (bf16[256,512]{0,1:T(8,128)(2,1)S(1)}, bf16[256,512]{0,1:T(8,128)(2,1)S(1)}, u32[]{:S(2)}, u32[]{:S(2)}) collective-permute-start(bf16[256,512]{0,1:T(8,128)(2,1)S(1)} %copy.126), channel_id=1, source_target_pairs={{0,2},{2,4},{4,6},{6,8},{8,10},{10,12},{12,14},{14,16},{16,18},{18... | collective-permute-start | bytes 786440 | tf_op jit(solution)/shard_map/while/body/eval_jaxpr/ppermute | solution.py:16
  466.3 17.5 %collective-permute-start.2 = (bf16[256,512]{0,1:T(8,128)(2,1)S(1)}, bf16[256,512]{0,1:T(8,128)(2,1)}, u32[]{:S(2)}, u32[]{:S(2)}) collective-permute-start(bf16[256,512]{0,1:T(8,128)(2,1)S(1)} %convert_element_type.500), channel_id=1, source_target_pairs={{0,2},{2,4},{4,6},{6,8},{8,10},{10,12},{12,14},{14,16},{16,18},{18... | collective-permute-start | bytes 786440 | tf_op jit(solution)/shard_map/while/body/eval_jaxpr/ppermute | solution.py:21
  468.7 16.8 %collective-permute-start.3 = (bf16[256,512]{0,1:T(8,128)(2,1)}, bf16[256,512]{0,1:T(8,128)(2,1)S(1)}, u32[]{:S(2)}, u32[]{:S(2)}) collective-permute-start(bf16[256,512]{0,1:T(8,128)(2,1)} %convert_element_type.502), channel_id=1, source_target_pairs={{0,2},{2,4},{4,6},{6,8},{8,10},{10,12},{12,14},{14,16},{16,18},{18... | collective-permute-start | bytes 786440 | tf_op jit(solution)/shard_map/while/body/eval_jaxpr/ppermute | solution.py:21
  471.1 15.3 %collective-permute-start = (bf16[256,512]{0,1:T(8,128)(2,1)S(1)}, bf16[256,512]{0,1:T(8,128)(2,1)S(1)}, u32[]{:S(2)}, u32[]{:S(2)}) collective-permute-start(bf16[256,512]{0,1:T(8,128)(2,1)S(1)} %copy.126), channel_id=1, source_target_pairs={{0,2},{2,4},{4,6},{6,8},{8,10},{10,12},{12,14},{14,16},{16,18},{18... | collective-permute-start | bytes 786440 | tf_op jit(solution)/shard_map/while/body/eval_jaxpr/ppermute | solution.py:16
  473.6 12.7 collective-permute-start.1
  494.2 12.5 collective-permute-start.2
  496.6 11.9 collective-permute-start.3
  499.0 10.4 collective-permute-start
  517.2 13.8 collective-permute-start.2
  520.8 11.9 collective-permute-start.3
  523.1 10.4 collective-permute-start
  541.3 17.5 %collective-permute-start.2 = (bf16[256,512]{0,1:T(8,128)(2,1)S(1)}, bf16[256,512]{0,1:T(8,128)(2,1)}, u32[]{:S(2)}, u32[]{:S(2)}) collective-permute-start(bf16[256,512]{0,1:T(8,128)(2,1)S(1)} %convert_element_type.500), channel_id=1, source_target_pairs={{0,2},{2,4},{4,6},{6,8},{8,10},{10,12},{12,14},{14,16},{16,18},{18... | collective-permute-start | bytes 786440 | tf_op jit(solution)/shard_map/while/body/eval_jaxpr/ppermute | solution.py:21
  543.8 16.8 %collective-permute-start.3 = (bf16[256,512]{0,1:T(8,128)(2,1)}, bf16[256,512]{0,1:T(8,128)(2,1)S(1)}, u32[]{:S(2)}, u32[]{:S(2)}) collective-permute-start(bf16[256,512]{0,1:T(8,128)(2,1)} %convert_element_type.502), channel_id=1, source_target_pairs={{0,2},{2,4},{4,6},{6,8},{8,10},{10,12},{12,14},{14,16},{16,18},{18... | collective-permute-start | bytes 786440 | tf_op jit(solution)/shard_map/while/body/eval_jaxpr/ppermute | solution.py:21
  550.0 11.4 collective-permute-start
  569.3 17.4 %collective-permute-start.2 = (bf16[256,512]{0,1:T(8,128)(2,1)S(1)}, bf16[256,512]{0,1:T(8,128)(2,1)}, u32[]{:S(2)}, u32[]{:S(2)}) collective-permute-start(bf16[256,512]{0,1:T(8,128)(2,1)S(1)} %convert_element_type.500), channel_id=1, source_target_pairs={{0,2},{2,4},{4,6},{6,8},{8,10},{10,12},{12,14},{14,16},{16,18},{18... | collective-permute-start | bytes 786440 | tf_op jit(solution)/shard_map/while/body/eval_jaxpr/ppermute | solution.py:21
  571.7 16.8 %collective-permute-start.3 = (bf16[256,512]{0,1:T(8,128)(2,1)}, bf16[256,512]{0,1:T(8,128)(2,1)S(1)}, u32[]{:S(2)}, u32[]{:S(2)}) collective-permute-start(bf16[256,512]{0,1:T(8,128)(2,1)} %convert_element_type.502), channel_id=1, source_target_pairs={{0,2},{2,4},{4,6},{6,8},{8,10},{10,12},{12,14},{14,16},{16,18},{18... | collective-permute-start | bytes 786440 | tf_op jit(solution)/shard_map/while/body/eval_jaxpr/ppermute | solution.py:21
  574.1 15.2 %collective-permute-start = (bf16[256,512]{0,1:T(8,128)(2,1)S(1)}, bf16[256,512]{0,1:T(8,128)(2,1)S(1)}, u32[]{:S(2)}, u32[]{:S(2)}) collective-permute-start(bf16[256,512]{0,1:T(8,128)(2,1)S(1)} %copy.126), channel_id=1, source_target_pairs={{0,2},{2,4},{4,6},{6,8},{8,10},{10,12},{12,14},{14,16},{16,18},{18... | collective-permute-start | bytes 786440 | tf_op jit(solution)/shard_map/while/body/eval_jaxpr/ppermute | solution.py:16
  597.1 16.5 %collective-permute-start.2 = (bf16[256,512]{0,1:T(8,128)(2,1)S(1)}, bf16[256,512]{0,1:T(8,128)(2,1)}, u32[]{:S(2)}, u32[]{:S(2)}) collective-permute-start(bf16[256,512]{0,1:T(8,128)(2,1)S(1)} %convert_element_type.500), channel_id=1, source_target_pairs={{0,2},{2,4},{4,6},{6,8},{8,10},{10,12},{12,14},{14,16},{16,18},{18... | collective-permute-start | bytes 786440 | tf_op jit(solution)/shard_map/while/body/eval_jaxpr/ppermute | solution.py:21
  599.5 15.9 %collective-permute-start.3 = (bf16[256,512]{0,1:T(8,128)(2,1)}, bf16[256,512]{0,1:T(8,128)(2,1)S(1)}, u32[]{:S(2)}, u32[]{:S(2)}) collective-permute-start(bf16[256,512]{0,1:T(8,128)(2,1)} %convert_element_type.502), channel_id=1, source_target_pairs={{0,2},{2,4},{4,6},{6,8},{8,10},{10,12},{12,14},{14,16},{16,18},{18... | collective-permute-start | bytes 786440 | tf_op jit(solution)/shard_map/while/body/eval_jaxpr/ppermute | solution.py:21
  601.9 14.3 collective-permute-start
  604.5 11.7 collective-permute-start.1
  624.0 13.6 collective-permute-start.2
  627.5 12.0 collective-permute-start.3
  629.8 10.4 collective-permute-start
  648.0 13.7 collective-permute-start.2
  651.6 12.7 collective-permute-start.3
  654.0 11.1 collective-permute-start
  656.6 8.5 collective-permute-start.1
  672.9 16.7 %collective-permute-start.2 = (bf16[256,512]{0,1:T(8,128)(2,1)S(1)}, bf16[256,512]{0,1:T(8,128)(2,1)}, u32[]{:S(2)}, u32[]{:S(2)}) collective-permute-start(bf16[256,512]{0,1:T(8,128)(2,1)S(1)} %convert_element_type.500), channel_id=1, source_target_pairs={{0,2},{2,4},{4,6},{6,8},{8,10},{10,12},{12,14},{14,16},{16,18},{18... | collective-permute-start | bytes 786440 | tf_op jit(solution)/shard_map/while/body/eval_jaxpr/ppermute | solution.py:21
  674.6 16.8 %collective-permute-start.3 = (bf16[256,512]{0,1:T(8,128)(2,1)}, bf16[256,512]{0,1:T(8,128)(2,1)S(1)}, u32[]{:S(2)}, u32[]{:S(2)}) collective-permute-start(bf16[256,512]{0,1:T(8,128)(2,1)} %convert_element_type.502), channel_id=1, source_target_pairs={{0,2},{2,4},{4,6},{6,8},{8,10},{10,12},{12,14},{14,16},{16,18},{18... | collective-permute-start | bytes 786440 | tf_op jit(solution)/shard_map/while/body/eval_jaxpr/ppermute | solution.py:21
  679.9 12.4 collective-permute-start
  700.1 17.4 %collective-permute-start.2 = (bf16[256,512]{0,1:T(8,128)(2,1)S(1)}, bf16[256,512]{0,1:T(8,128)(2,1)}, u32[]{:S(2)}, u32[]{:S(2)}) collective-permute-start(bf16[256,512]{0,1:T(8,128)(2,1)S(1)} %convert_element_type.500), channel_id=1, source_target_pairs={{0,2},{2,4},{4,6},{6,8},{8,10},{10,12},{12,14},{14,16},{16,18},{18... | collective-permute-start | bytes 786440 | tf_op jit(solution)/shard_map/while/body/eval_jaxpr/ppermute | solution.py:21
  702.5 16.8 %collective-permute-start.3 = (bf16[256,512]{0,1:T(8,128)(2,1)}, bf16[256,512]{0,1:T(8,128)(2,1)S(1)}, u32[]{:S(2)}, u32[]{:S(2)}) collective-permute-start(bf16[256,512]{0,1:T(8,128)(2,1)} %convert_element_type.502), channel_id=1, source_target_pairs={{0,2},{2,4},{4,6},{6,8},{8,10},{10,12},{12,14},{14,16},{16,18},{18... | collective-permute-start | bytes 786440 | tf_op jit(solution)/shard_map/while/body/eval_jaxpr/ppermute | solution.py:21
  704.9 15.2 %collective-permute-start = (bf16[256,512]{0,1:T(8,128)(2,1)S(1)}, bf16[256,512]{0,1:T(8,128)(2,1)S(1)}, u32[]{:S(2)}, u32[]{:S(2)}) collective-permute-start(bf16[256,512]{0,1:T(8,128)(2,1)S(1)} %copy.126), channel_id=1, source_target_pairs={{0,2},{2,4},{4,6},{6,8},{8,10},{10,12},{12,14},{14,16},{16,18},{18... | collective-permute-start | bytes 786440 | tf_op jit(solution)/shard_map/while/body/eval_jaxpr/ppermute | solution.py:16
  727.9 15.5 %collective-permute-start.2 = (bf16[256,512]{0,1:T(8,128)(2,1)S(1)}, bf16[256,512]{0,1:T(8,128)(2,1)}, u32[]{:S(2)}, u32[]{:S(2)}) collective-permute-start(bf16[256,512]{0,1:T(8,128)(2,1)S(1)} %convert_element_type.500), channel_id=1, source_target_pairs={{0,2},{2,4},{4,6},{6,8},{8,10},{10,12},{12,14},{14,16},{16,18},{18... | collective-permute-start | bytes 786440 | tf_op jit(solution)/shard_map/while/body/eval_jaxpr/ppermute | solution.py:21
  730.4 15.3 %collective-permute-start.3 = (bf16[256,512]{0,1:T(8,128)(2,1)}, bf16[256,512]{0,1:T(8,128)(2,1)S(1)}, u32[]{:S(2)}, u32[]{:S(2)}) collective-permute-start(bf16[256,512]{0,1:T(8,128)(2,1)} %convert_element_type.502), channel_id=1, source_target_pairs={{0,2},{2,4},{4,6},{6,8},{8,10},{10,12},{12,14},{14,16},{16,18},{18... | collective-permute-start | bytes 786440 | tf_op jit(solution)/shard_map/while/body/eval_jaxpr/ppermute | solution.py:21
  732.7 13.8 collective-permute-start
  735.3 11.2 collective-permute-start.1
  754.3 16.6 %collective-permute-start.2 = (bf16[256,512]{0,1:T(8,128)(2,1)S(1)}, bf16[256,512]{0,1:T(8,128)(2,1)}, u32[]{:S(2)}, u32[]{:S(2)}) collective-permute-start(bf16[256,512]{0,1:T(8,128)(2,1)S(1)} %convert_element_type.500), channel_id=1, source_target_pairs={{0,2},{2,4},{4,6},{6,8},{8,10},{10,12},{12,14},{14,16},{16,18},{18... | collective-permute-start | bytes 786440 | tf_op jit(solution)/shard_map/while/body/eval_jaxpr/ppermute | solution.py:21
  758.3 15.3 %collective-permute-start.3 = (bf16[256,512]{0,1:T(8,128)(2,1)}, bf16[256,512]{0,1:T(8,128)(2,1)S(1)}, u32[]{:S(2)}, u32[]{:S(2)}) collective-permute-start(bf16[256,512]{0,1:T(8,128)(2,1)} %convert_element_type.502), channel_id=1, source_target_pairs={{0,2},{2,4},{4,6},{6,8},{8,10},{10,12},{12,14},{14,16},{16,18},{18... | collective-permute-start | bytes 786440 | tf_op jit(solution)/shard_map/while/body/eval_jaxpr/ppermute | solution.py:21
  760.7 13.8 collective-permute-start
  763.2 11.2 collective-permute-start.1
  779.9 143.2 %all-reduce.24.cloned.1.call-start = ((), (), s32[]{:S(2)}) async-start(), calls=%async_computation.8 | async-start | bytes 1572864 | tf_op jit(solution)/shard_map/psum | solution.py:53
  892.1 547.5 %all-reduce.22.cloned.1.call-start = ((), (), s32[]{:S(2)}) async-start(), calls=%async_computation.7 | async-start | bytes 58720256 | tf_op jit(solution)/shard_map/psum | solution.py:330
  (154 other events, 1373.6 us)
Sparse Core Ops, SparseCore 0:
  12.8 53.4 all-gather.2
  69.0 49.0 all-gather.4
  184.6 27.0 all-reduce.11
  225.2 28.5 all-reduce.13
  272.1 28.5 all-reduce.15
  314.8 28.5 all-reduce.17
  780.0 36.5 all-reduce.19
  892.2 30.8 all-reduce.23
  930.1 509.5 all-reduce.21
where the time goes:
time: 1480 us; the launch traced here: 1470 us
  waiting for transfers between devices  750 us (51%)
  starting transfers between devices  234 us (16%)
  local copies, waits for them, and re-layouts  142 us (10%)
  other arithmetic  127 us (9%)
  matrix products  109 us (7%)
  blocking collectives  67.9 us (5%)
  loops' own time  23.5 us (2%)
  between operations  16.5 us (1%)
    psum x1, waiting for transfers between devices, shards(): lax.psum((grad_query_weight, grad_key_weight, grad_value_weight, grad_out...  513 us
    ppermute x32, starting transfers between devices, shifted(): return lax.ppermute(block, axis, route)  149 us
    psum x6, waiting for transfers between devices, head_sum(): return lax.psum(values.astype(jnp.bfloat16), 'tp').astype(jnp.float32)  134 us
    ppermute x32, starting transfers between devices, shifted_2(): lax.ppermute(value, axis, [(i, (i + by) % size) for i in range(size)])  83.7 us
    psum x1, blocking collectives, shards(): lax.psum((text_key_part.reshape(text_count, width_here), text_value_part....  67.9 us
    dot_general x30, matrix products, matmul(): return jnp.dot(left, right, preferred_element_type=jnp.float32)  66.9 us
    all_gather x1, waiting for transfers between devices, shards(): value_piece = lax.all_gather(values, 'blk', axis=0, tiled=True)  51.8 us
    all_gather x1, waiting for transfers between devices, shards(): key_piece = lax.all_gather(keys, 'blk', axis=0, tiled=True)  44.4 us
  transfers between devices with their start and end apart: 73, of which 15 were waited for; matrix products, arithmetic and copies ran while one was open for 7% of the time, Pallas kernels for 0%

commit v1 on v0

v1 whole, which is shorter than its diff:
```python
import functools
import jax
import jax.numpy as jnp
from jax import lax
from jax.experimental import pallas as pl
from jax.experimental.pallas import tpu as pltpu
from jax.sharding import PartitionSpec as P

HEAD_DIM = 64
NEGATIVE = -1e30
BF, F32 = jnp.bfloat16, jnp.float32


def dg(left, right, dims):
    return lax.dot_general(left, right, (dims, ((), ())), preferred_element_type=F32)


def tile_ranges(positions, first, tile, chunk):
    rows = positions.reshape(-1, tile)
    starts = first.reshape(-1, tile)
    low = jnp.min(starts, axis=1) // chunk
    high = jnp.max(rows, axis=1) // chunk + 1
    clear = jnp.clip((jnp.max(starts, axis=1) + chunk - 1) // chunk, low, high)
    stop = jnp.clip((jnp.min(rows, axis=1) + 1) // chunk, clear, high)
    return jnp.stack([low, clear, stop, high], axis=1)


def allowed_keys(base, flip, chunk, rows, first):
    keys = (base + lax.broadcasted_iota(jnp.int32, (chunk, rows.shape[1]), 0)) ^ flip
    return (keys <= rows) & (keys >= first)


def attend_kernel(ranges, flips, q_ref, k_ref, v_ref, row_ref, first_ref, out_ref, log_ref, k_rows, chunk):
    tile = pl.program_id(0)
    total = k_ref.shape[1]

    @pl.when(tile == 0)
    def _():
        for base in range(0, total, chunk):
            k_rows[base : base + chunk, :] = k_ref[:, base : base + chunk].T

    queries = q_ref[...]
    rows, first = row_ref[...], first_ref[...]
    width = queries.shape[1]

    def work(masked):
        def step(index, carry):
            best, total_weight, acc = carry
            base = pl.multiple_of(index * chunk, chunk)
            score = jnp.dot(k_rows[pl.ds(base, chunk), :], queries, preferred_element_type=F32)
            if masked:
                allowed = allowed_keys(base, flips[0], chunk, rows, first)
                score = jnp.where(allowed, score, NEGATIVE)
            new_best = jnp.maximum(best, jnp.max(score, axis=0, keepdims=True))
            expo = jnp.exp(score - new_best)
            if masked:
                expo = jnp.where(allowed, expo, 0.0)
            fade = jnp.exp(best - new_best)
            total_weight = total_weight * fade + jnp.sum(expo, axis=0, keepdims=True)
            acc = acc * fade + jnp.dot(
                v_ref[:, pl.ds(base, chunk)], expo.astype(BF), preferred_element_type=F32
            )
            return new_best, total_weight, acc

        return step

    carry = (
        jnp.full((1, width), NEGATIVE, F32),
        jnp.zeros((1, width), F32),
        jnp.zeros((HEAD_DIM, width), F32),
    )
    carry = lax.fori_loop(ranges[tile, 0], ranges[tile, 1], work(True), carry)
    carry = lax.fori_loop(ranges[tile, 1], ranges[tile, 2], work(False), carry)
    best, total_weight, acc = lax.fori_loop(ranges[tile, 2], ranges[tile, 3], work(True), carry)
    out_ref[...] = acc / total_weight
    log_ref[...] = best + jnp.log(total_weight)


def attend(queries, keys, values, rows, first, flip, tile=512, chunk=1024):
    count, total = queries.shape[1], keys.shape[1]
    tile = min(tile, count)
    chunk = min(chunk, total)
    ranges = tile_ranges(rows, first, tile, chunk)
    whole = lambda i, r, f: (0, 0)
    part = lambda i, r, f: (0, i)
    return pl.pallas_call(
        functools.partial(attend_kernel, chunk=chunk),
        grid_spec=pltpu.PrefetchScalarGridSpec(
            num_scalar_prefetch=2,
            grid=(count // tile,),
            in_specs=[
                pl.BlockSpec((HEAD_DIM, tile), part),
                pl.BlockSpec((HEAD_DIM, total), whole),
                pl.BlockSpec((HEAD_DIM, total), whole),
                pl.BlockSpec((1, tile), part),
                pl.BlockSpec((1, tile), part),
            ],
            out_specs=[pl.BlockSpec((HEAD_DIM, tile), part), pl.BlockSpec((1, tile), part)],
            scratch_shapes=[pltpu.VMEM((total, HEAD_DIM), BF)],
        ),
        out_shape=[
            jax.ShapeDtypeStruct((HEAD_DIM, count), F32),
            jax.ShapeDtypeStruct((1, count), F32),
        ],
        compiler_params=pltpu.CompilerParams(vmem_limit_bytes=40 << 20),
        name="attend",
    )(ranges, flip.reshape(1), queries, keys, values, rows.reshape(1, -1), first.reshape(1, -1))


def attend_back_kernel(
    ranges, flips, q_ref, k_ref, v_ref, row_ref, first_ref, out_ref, log_ref, do_ref,
    dq_ref, dk_ref, dv_ref, k_rows, v_rows, chunk,
):
    tile = pl.program_id(0)
    total = k_ref.shape[1]

    @pl.when(tile == 0)
    def _():
        for base in range(0, total, chunk):
            k_rows[base : base + chunk, :] = k_ref[:, base : base + chunk].T
            v_rows[base : base + chunk, :] = v_ref[:, base : base + chunk].T
        dk_ref[...] = jnp.zeros_like(dk_ref)
        dv_ref[...] = jnp.zeros_like(dv_ref)

    queries, grads = q_ref[...], do_ref[...]
    rows, first = row_ref[...], first_ref[...]
    log_total = log_ref[...]
    delta = jnp.sum(grads.astype(F32) * out_ref[...], axis=0, keepdims=True)

    def work(masked):
        def step(index, acc):
            base = pl.multiple_of(index * chunk, chunk)
            span = pl.ds(base, chunk)
            score = jnp.dot(k_rows[span, :], queries, preferred_element_type=F32)
            weights = jnp.exp(score - log_total)
            if masked:
                allowed = allowed_keys(base, flips[0], chunk, rows, first)
                weights = jnp.where(allowed, weights, 0.0)
            grad_weights = jnp.dot(v_rows[span, :], grads, preferred_element_type=F32)
            grad_score = (weights * (grad_weights - delta)).astype(BF)
            dv_ref[:, span] += dg(grads, weights.astype(BF), ((1,), (1,)))
            dk_ref[:, span] += dg(queries, grad_score, ((1,), (1,)))
            return acc + jnp.dot(k_ref[:, span], grad_score, preferred_element_type=F32)

        return step

    acc = jnp.zeros(queries.shape, F32)
    acc = lax.fori_loop(ranges[tile, 0], ranges[tile, 1], work(True), acc)
    acc = lax.fori_loop(ranges[tile, 1], ranges[tile, 2], work(False), acc)
    dq_ref[...] = lax.fori_loop(ranges[tile, 2], ranges[tile, 3], work(True), acc).astype(BF)


def attend_back(queries, keys, values, rows, first, flip, out, log_total, grads, tile=512, chunk=1024):
    count, total = queries.shape[1], keys.shape[1]
    tile = min(tile, count)
    chunk = min(chunk, total)
    ranges = tile_ranges(rows, first, tile, chunk)
    whole = lambda i, r, f: (0, 0)
    part = lambda i, r, f: (0, i)
    return pl.pallas_call(
        functools.partial(attend_back_kernel, chunk=chunk),
        grid_spec=pltpu.PrefetchScalarGridSpec(
            num_scalar_prefetch=2,
            grid=(count // tile,),
            in_specs=[
                pl.BlockSpec((HEAD_DIM, tile), part),
                pl.BlockSpec((HEAD_DIM, total), whole),
                pl.BlockSpec((HEAD_DIM, total), whole),
                pl.BlockSpec((1, tile), part),
                pl.BlockSpec((1, tile), part),
                pl.BlockSpec((HEAD_DIM, tile), part),
                pl.BlockSpec((1, tile), part),
                pl.BlockSpec((HEAD_DIM, tile), part),
            ],
            out_specs=[
                pl.BlockSpec((HEAD_DIM, tile), part),
                pl.BlockSpec((HEAD_DIM, total), whole),
                pl.BlockSpec((HEAD_DIM, total), whole),
            ],
            scratch_shapes=[pltpu.VMEM((total, HEAD_DIM), BF), pltpu.VMEM((total, HEAD_DIM), BF)],
        ),
        out_shape=[
            jax.ShapeDtypeStruct((HEAD_DIM, count), BF),
            jax.ShapeDtypeStruct((HEAD_DIM, total), F32),
            jax.ShapeDtypeStruct((HEAD_DIM, total), F32),
        ],
        compiler_params=pltpu.CompilerParams(vmem_limit_bytes=48 << 20),
        name="attend_back",
    )(ranges, flip.reshape(1), queries, keys, values, rows.reshape(1, -1), first.reshape(1, -1), out, log_total, grads)


EPSILON = 1e-05
SWAP = [(0, 1), (1, 0)]


def over_x(value):
    return lax.ppermute(value, "tp", SWAP)


def over_blk(value, bit):
    return lax.ppermute(value, "blk", [(i, i ^ bit) for i in range(lax.axis_size("blk"))])


def normalize(values):
    centre = values - jnp.mean(values, axis=-1, keepdims=True)
    spread = lax.rsqrt(jnp.mean(centre * centre, axis=-1, keepdims=True) + EPSILON)
    return centre * spread, spread


def norm_back(values, gain, grad):
    hat, spread = normalize(values)
    scaled = grad * gain
    through = spread * (
        scaled
        - jnp.mean(scaled, axis=-1, keepdims=True)
        - hat * jnp.mean(scaled * hat, axis=-1, keepdims=True)
    )
    return through, jnp.sum(grad * hat, axis=0), jnp.sum(grad, axis=0)


def clip_rows(positions, clip_lengths):
    index = jnp.arange(clip_lengths.shape[0], dtype=jnp.int32)
    starts = jnp.sum(jnp.where(index[None, :] < index[:, None], clip_lengths[None, :], 0), axis=1)
    ends = starts + clip_lengths
    segment = jnp.sum((positions[:, None] >= ends[None, :]).astype(jnp.int32), axis=1)
    match = segment[:, None] == index[None, :]
    first = jnp.sum(jnp.where(match, starts[None, :], 0), axis=1)
    return segment, first


def matmul(left, right):
    return jnp.dot(left, right, preferred_element_type=F32)


def matmul_nt(left, right):
    return dg(left, right, ((1,), (1,)))


def matmul_tn(left, right):
    return dg(left, right, ((0,), (0,)))


def other_half(weight, core):
    rows = weight.shape[0] // 2
    sent = lax.dynamic_slice_in_dim(weight, core * rows, rows, 0)
    got = over_x(sent)
    more = over_blk(got, 1)
    return jnp.concatenate([jnp.where(core == 0, got, more), jnp.where(core == 0, more, got)])


def in_order(own, other, tp):
    return jnp.concatenate([jnp.where(tp == 0, own, other), jnp.where(tp == 0, other, own)])


def shards(
    frames,
    clip_lengths,
    text_states,
    text_segments,
    gain_one,
    shift_one,
    gain_two,
    shift_two,
    gain_three,
    shift_three,
    query_weight,
    key_weight,
    value_weight,
    output_weight,
    cross_query,
    cross_key,
    cross_value,
    cross_output,
    inner_weight,
    outer_weight,
    cotangent,
):
    row_count = frames.shape[0]
    width_here = query_weight.shape[1]
    heads_here = width_here // HEAD_DIM
    blk_count, tp_count = lax.axis_size("blk"), lax.axis_size("tp")
    blk, tp = lax.axis_index("blk"), lax.axis_index("tp")
    core = blk % 2
    copies = blk_count // heads_here
    sub = row_count // copies
    half = row_count // tp_count
    mine = blk % copies
    scale = float(HEAD_DIM) ** (-0.5)

    def own_rows(array):
        return lax.dynamic_slice_in_dim(array, tp * half, half, 0)

    def other_rows(array):
        return lax.dynamic_slice_in_dim(array, (1 - tp) * half, half, 0)

    inputs = frames.astype(F32)
    hat, _ = normalize(inputs)
    normed_one = (hat * gain_one + shift_one).astype(BF)
    q_t = (dg(query_weight, normed_one, ((0,), (1,))) * scale).astype(BF)
    k_t = dg(key_weight, normed_one, ((0,), (1,))).astype(BF)
    v_t = dg(value_weight, normed_one, ((0,), (1,))).astype(BF)

    weights_two = [output_weight, cross_query, cross_output]
    output_both, query_both, cross_both = [[w, other_half(w, core)] for w in weights_two]
    text_k = matmul(text_states, cross_key).astype(BF)
    text_v = matmul(text_states, cross_value).astype(BF)
    text_other = over_x(jnp.stack([text_k, text_v]))
    text_keys, text_values = [text_k, text_other[0]], [text_v, text_other[1]]

    def spread_heads(array):
        count = array.shape[0]
        array = array.reshape(count, heads_here, HEAD_DIM, copies, sub).transpose(1, 3, 0, 2, 4)
        return lax.all_to_all(
            array.reshape(blk_count, count, HEAD_DIM, sub), "blk", 0, 0, tiled=True
        )

    def bring_heads(array):
        got = lax.all_to_all(array, "blk", 0, 0, tiled=True)
        return got.reshape(heads_here, copies, array.shape[1], HEAD_DIM, sub)

    got = spread_heads(jnp.stack([q_t, k_t, v_t]))
    queries = got[:, 0].transpose(1, 0, 2).reshape(HEAD_DIM, blk_count * sub)
    both = got[:, 1:][:, :, :, None, :]
    bit = 1
    while bit < copies:
        both = jnp.concatenate([both, over_blk(both, bit)], axis=3)
        bit *= 2
    both = both.transpose(1, 2, 0, 3, 4).reshape(2, HEAD_DIM, blk_count * row_count)
    keys, values = both[0], both[1]
    rows_all = jnp.arange(blk_count, dtype=jnp.int32)[:, None] * row_count
    rows_all = (rows_all + mine * sub + jnp.arange(sub, dtype=jnp.int32)[None, :]).reshape(-1)
    _, first = clip_rows(rows_all, clip_lengths)
    flip = mine * sub
    out, log_total = attend(queries, keys, values, rows_all, first, flip)
    out_low = out.astype(BF).reshape(HEAD_DIM, blk_count, sub).transpose(1, 0, 2)[:, None]
    attended = bring_heads(out_low)[:, :, 0]

    def token_half(array, which):
        array = array.reshape(heads_here, tp_count, copies // tp_count, HEAD_DIM, sub)
        array = lax.dynamic_index_in_dim(array, which, 1, keepdims=False)
        return array.transpose(0, 2, 1, 3).reshape(width_here, half)

    a_own, a_sent = token_half(attended, tp), token_half(attended, 1 - tp)
    a_both = [a_own, over_x(a_sent)]

    rows = blk * row_count + tp * half + jnp.arange(half, dtype=jnp.int32)
    segment, _ = clip_rows(rows, clip_lengths)
    x_own = own_rows(frames).astype(F32)
    first_sum = x_own + matmul_tn(a_both[0], output_both[0]) + matmul_tn(a_both[1], output_both[1])
    hat, _ = normalize(first_sum)
    normed_two = (hat * gain_two + shift_two).astype(BF)
    allowed_text = text_segments[:, None] == segment[None, :]
    second_sum = first_sum
    crossed, cross_outs, cross_weights, cross_qs = [], [], [], []
    for side in range(2):
        qc = (matmul(normed_two, query_both[side]) * scale).astype(BF)
        qh = qc.reshape(half, heads_here, HEAD_DIM)
        kh = text_keys[side].reshape(-1, heads_here, HEAD_DIM)
        vh = text_values[side].reshape(-1, heads_here, HEAD_DIM)
        score = jnp.einsum("khd,qhd->hkq", kh, qh, preferred_element_type=F32)
        score = jnp.where(allowed_text[None], score, NEGATIVE)
        expo = jnp.exp(score - jnp.max(score, axis=1, keepdims=True))
        expo = jnp.where(allowed_text[None], expo, 0.0)
        weights = expo / jnp.sum(expo, axis=1, keepdims=True)
        oc = jnp.einsum("hkq,khd->qhd", weights.astype(BF), vh, preferred_element_type=F32)
        c = oc.reshape(half, width_here).astype(BF)
        second_sum = second_sum + matmul(c, cross_both[side])
        crossed.append(c), cross_outs.append(oc), cross_weights.append(weights), cross_qs.append(qh)
    hat, _ = normalize(second_sum)
    h3_own = (hat * gain_three + shift_three).astype(BF)

    h3_all = jnp.concatenate([h3_own, over_x(h3_own)])
    dy_own = own_rows(cotangent)
    dy_all = jnp.concatenate([dy_own, other_rows(cotangent)])
    hidden_pre = matmul(h3_all, inner_weight)
    hidden_grad = matmul_nt(dy_all, outer_weight)
    cdf = 0.5 * (1.0 + lax.erf(hidden_pre * (0.5**0.5)))
    density = jnp.exp(-0.5 * hidden_pre * hidden_pre) * 0.3989422804014327
    hidden = (hidden_pre * cdf).astype(BF)
    grad_pre = (hidden_grad * (cdf + hidden_pre * density)).astype(BF)
    dh3 = matmul_nt(grad_pre, inner_weight).astype(BF)
    dh3_own = dh3[:half].astype(F32) + over_x(dh3[half:]).astype(F32)
    y = matmul(hidden, outer_weight)
    y_own = second_sum + y[:half] + over_x(y[half:].astype(BF)).astype(F32)
    y_own = y_own.astype(BF)
    result = in_order(y_own, over_x(y_own), tp)
    grad_outer = matmul_tn(hidden, dy_all).astype(BF)
    grad_inner = matmul_tn(h3_all, grad_pre).astype(BF)

    through, grad_gain_three, grad_shift_three = norm_back(second_sum, gain_three, dh3_own)
    dx2 = dy_own.astype(F32) + through
    dx2_low = dx2.astype(BF)
    dh2 = 0.0
    dqcs, dk_parts, dv_parts = [], [], []
    for side in range(2):
        kh = text_keys[side].reshape(-1, heads_here, HEAD_DIM)
        vh = text_values[side].reshape(-1, heads_here, HEAD_DIM)
        dc = matmul_nt(dx2_low, cross_both[side]).astype(BF).reshape(half, heads_here, HEAD_DIM)
        delta = jnp.sum(dc.astype(F32) * cross_outs[side], axis=-1).T
        dweights = jnp.einsum("khd,qhd->hkq", vh, dc, preferred_element_type=F32)
        dscore = (cross_weights[side] * (dweights - delta[:, None, :])).astype(BF)
        dqc = jnp.einsum("hkq,khd->qhd", dscore, kh, preferred_element_type=F32).astype(BF)
        dqc = (dqc * scale).reshape(half, width_here)
        dk_parts.append(jnp.einsum("hkq,qhd->khd", dscore, cross_qs[side], preferred_element_type=F32))
        dv_parts.append(
            jnp.einsum("hkq,qhd->khd", cross_weights[side].astype(BF), dc, preferred_element_type=F32)
        )
        dh2 = dh2 + matmul_nt(dqc, query_both[side])
        dqcs.append(dqc)
    through, grad_gain_two, grad_shift_two = norm_back(first_sum, gain_two, dh2)
    dx1 = dx2 + through
    dx1_low = dx1.astype(BF)
    da_t = [dg(w, dx1_low, ((1,), (1,))).astype(BF) for w in output_both]
    da_other = over_x(da_t[1])

    def as_heads(array):
        return array.reshape(heads_here, HEAD_DIM, copies // tp_count, sub).transpose(0, 2, 1, 3)

    low = jnp.where(tp == 0, as_heads(da_t[0]), as_heads(da_other))
    high = jnp.where(tp == 0, as_heads(da_other), as_heads(da_t[0]))
    sent = jnp.concatenate([low, high], axis=1).reshape(blk_count, 1, HEAD_DIM, sub)
    grads = lax.all_to_all(sent, "blk", 0, 0, tiled=True)[:, 0]
    grads = grads.transpose(1, 0, 2).reshape(HEAD_DIM, blk_count * sub)
    dq, dk, dv = attend_back(queries, keys, values, rows_all, first, flip, out, log_total, grads)
    parts = jnp.stack([dk, dv]).reshape(2, HEAD_DIM, blk_count, copies, sub)
    bit = copies // 2
    while bit:
        split = parts.reshape(2, HEAD_DIM, blk_count, 2, bit, sub)
        parts = split[:, :, :, 0] + over_blk(split[:, :, :, 1].astype(BF), bit).astype(F32)
        bit //= 2
    parts = parts.reshape(2, HEAD_DIM, blk_count, sub).transpose(2, 0, 1, 3).astype(BF)
    dq_part = dq.reshape(HEAD_DIM, blk_count, sub).transpose(1, 0, 2)[:, None]
    back = bring_heads(jnp.concatenate([dq_part, parts], axis=1))
    back = back.transpose(2, 0, 3, 1, 4).reshape(3, width_here, row_count)
    dq_t, dk_t, dv_t = back[0] * jnp.asarray(scale, BF), back[1], back[2]
    dh1 = (
        dg(dq_t, query_weight, ((0,), (1,)))
        + dg(dk_t, key_weight, ((0,), (1,)))
        + dg(dv_t, value_weight, ((0,), (1,)))
    ).astype(BF)
    dh1_own = own_rows(dh1).astype(F32) + over_x(other_rows(dh1)).astype(F32)
    through, grad_gain_one, grad_shift_one = norm_back(x_own, gain_one, dh1_own)
    dx = (dx1 + through).astype(BF)
    grad_frames = in_order(dx, over_x(dx), tp)

    grad_query = dg(normed_one, dq_t, ((0,), (1,))).astype(BF)
    grad_key = dg(normed_one, dk_t, ((0,), (1,))).astype(BF)
    grad_value = dg(normed_one, dv_t, ((0,), (1,))).astype(BF)
    dx1_other = over_x(dx1_low)
    grad_output = (matmul(a_own, dx1_low) + matmul(a_sent, dx1_other)).astype(BF)
    dx2_other = over_x(dx2_low)
    c_other = over_x(crossed[1])
    grad_cross_output = (
        matmul_tn(crossed[0], dx2_low) + matmul_tn(c_other, dx2_other)
    ).astype(BF)
    h2_other = over_x(normed_two)
    dqc_other = over_x(dqcs[1])
    grad_cross_query = (matmul_tn(normed_two, dqcs[0]) + matmul_tn(h2_other, dqc_other)).astype(BF)

    parts = [jnp.stack([dk_parts[i], dv_parts[i]]).reshape(2, -1, width_here) for i in range(2)]
    text_part = parts[0] + over_x(parts[1].astype(BF)).astype(F32)
    text_total = lax.psum(text_part, "blk").astype(BF)
    grad_cross_key = matmul_tn(text_states, text_total[0])
    grad_cross_value = matmul_tn(text_states, text_total[1])
    grad_text = matmul_nt(text_total[0], cross_key) + matmul_nt(text_total[1], cross_value)
    grad_text = grad_text.astype(BF)
    grad_text = grad_text.astype(F32) + over_x(grad_text).astype(F32)

    small = jnp.stack(
        [grad_gain_one, grad_shift_one, grad_gain_two, grad_shift_two, grad_gain_three, grad_shift_three]
    )
    small = lax.psum(small, ("blk", "tp"))
    grads = [
        grad_query, grad_key, grad_value, grad_output, grad_cross_query, grad_cross_output,
        grad_inner, grad_outer,
    ]
    grads = [g.astype(F32) for g in lax.psum(grads, "blk")]
    return (
        result,
        grad_frames,
        grad_text,
        small[0],
        small[1],
        small[2],
        small[3],
        small[4],
        small[5],
        grads[0],
        grads[1],
        grads[2],
        grads[3],
        grads[4],
        grad_cross_key,
        grad_cross_value,
        grads[5],
        grads[6],
        grads[7],
    )


def solution(mesh):
    return jax.shard_map(
        shards,
        mesh=mesh,
        in_specs=(
            P("blk", None),
            P(),
            P(),
            P(),
            P(),
            P(),
            P(),
            P(),
            P(),
            P(),
            P(None, "tp"),
            P(None, "tp"),
            P(None, "tp"),
            P("tp", None),
            P(None, "tp"),
            P(None, "tp"),
            P(None, "tp"),
            P("tp", None),
            P(None, "tp"),
            P("tp", None),
            P("blk", None),
        ),
        out_specs=(
            P("blk", None),
            P("blk", None),
            P(),
            P(),
            P(),
            P(),
            P(),
            P(),
            P(),
            P(None, "tp"),
            P(None, "tp"),
            P(None, "tp"),
            P("tp", None),
            P(None, "tp"),
            P(None, "tp"),
            P(None, "tp"),
            P("tp", None),
            P(None, "tp"),
            P("tp", None),
        ),
        check_vma=False,
    )
```

time: 1480 us -> 581 us (0.39)
  waiting for transfers between devices: 750 us -> 207 us
  starting transfers between devices: 234 us -> 44.3 us
  local copies, waits for them, and re-layouts: 142 us -> 39.7 us
  other arithmetic: 127 us -> 46.2 us
  blocking collectives: 67.9 us -> 118 us
  matrix products: 109 us -> 74 us
  Pallas kernels: 0 us -> 31.4 us
  loops' own time: 23.5 us -> 0 us
    psum x7 -> x1, waiting for transfers between devices: 647 us -> 126 us  [shards(): grads = [g.astype(F32) for g in lax.psum(grads, 'blk')]]
    ppermute x64 -> x24, starting transfers between devices: 233 us -> 22 us  [the longest x19 21.3 us: over_x(): return lax.ppermute(value, 'tp', SWAP)]
    all_gather x2 -> x0, waiting for transfers between devices: 96.2 us -> none  [the longest x1 51.8 us: shards(): value_piece = lax.all_gather(values, 'blk', axis=0, tiled=True)]
    ppermute x64 -> x24, waiting for transfers between devices: 6.54 us -> 67.1 us  [the longest x19 67.1 us: over_x(): return lax.ppermute(value, 'tp', SWAP)]
    psum x1 -> x2, blocking collectives: 67.9 us -> 118 us  [the longest x1 78.7 us: shards(): text_total = lax.psum(text_part, 'blk').astype(BF)]
    while x128 -> x0, local copies, waits for them, and re-layouts: 39.7 us -> none
    slice x34 -> x9, local copies, waits for them, and re-layouts: 43.7 us -> 5.2 us  [the longest x3 3 us: shards(): keys, values = (both[0], both[1])]
    convert_element_type x71 -> x14, other arithmetic: 62.5 us -> 25.1 us  [the longest x8 20.8 us: shards(): grads = [g.astype(F32) for g in lax.psum(grads, 'blk')]]
  transfers between devices with their start and end apart: 73 -> 29, of which waited for: 15 -> 15; matrix products, arithmetic and copies ran while one was open for 7% -> 12% of each run, Pallas kernels for 0% -> 5%
where the time goes in v1:
time: 581 us; the launch traced here: 576 us
  waiting for transfers between devices  207 us (36%)
  blocking collectives  118 us (20%)
  matrix products  74 us (13%)
  other arithmetic  46.2 us (8%)
  starting transfers between devices  44.3 us (8%)
  local copies, waits for them, and re-layouts  39.7 us (7%)
  Pallas kernels  31.4 us (5%)
  between operations  15.7 us (3%)
    psum x1, waiting for transfers between devices, shards(): grads = [g.astype(F32) for g in lax.psum(grads, 'blk')]  126 us
    psum x1, blocking collectives, shards(): text_total = lax.psum(text_part, 'blk').astype(BF)  78.7 us
    ppermute x19, waiting for transfers between devices, over_x(): return lax.ppermute(value, 'tp', SWAP)  67.1 us
    dot_general x29, matrix products, dg(): lax.dot_general(left, right, (dims, ((), ())), preferred_element_type=F32)  43.7 us
    psum x1, blocking collectives, shards(): small = lax.psum(small, ('blk', 'tp'))  38.8 us
    ppermute x19, starting transfers between devices, over_x(): return lax.ppermute(value, 'tp', SWAP)  21.3 us
    convert_element_type x8, other arithmetic, shards(): grads = [g.astype(F32) for g in lax.psum(grads, 'blk')]  20.8 us
    pallas_call x1, Pallas kernels, attend_back(): pl.pallas_call(functools.partial(attend_back_kernel, chunk=chunk), grid_s...  17 us
  transfers between devices with their start and end apart: 29, of which 15 were waited for; matrix products, arithmetic and copies ran while one was open for 12% of the time, Pallas kernels for 5%

profile of v1, /device:TPU:0, one launch (start us, length us, event | category | flops | bytes accessed | tf_op | source)
XLA Modules:
  0.0 575.7 jit_solution(6636535872007424765)
XLA Ops:
  9.9 2.0 fusion.25
  12.9 1.7 fusion.24
  17.2 7.8 %all-to-all-start = ((bf16[16,3,64,128]{3,2,1,0:T(8,128)(2,1)}), bf16[16,3,64,128]{3,2,1,0:T(8,128)(2,1)}, u32[]{:S(2)}, u32[]{:S(2)}) async-start(bf16[16,3,64,128]{3,2,1,0:T(8,128)(2,1)} %bitcast.251), calls=%async_computation | async-start | bytes 1572864 | tf_op jit(solution)/shard_map/all_to_all | solution.py:313
  34.3 6.6 %collective-permute-done.2 = bf16[256,1024]{1,0:T(8,128)(2,1)} collective-permute-done((bf16[256,1024]{1,0:T(8,128)(2,1)}, bf16[256,1024]{1,0:T(8,128)(2,1)}, u32[]{:S(2)}, u32[]{:S(2)}) %collective-permute-start.2) | collective-permute-done | bytes 524320 | tf_op jit(solution)/shard_map/ppermute | solution.py:197
  42.5 15.2 %collective-permute-done.4 = bf16[2,128,512]{2,1,0:T(8,128)(2,1)S(1)} collective-permute-done((bf16[2,128,512]{2,1,0:T(8,128)(2,1)S(1)}, bf16[2,128,512]{2,1,0:T(8,128)(2,1)S(1)}, u32[]{:S(2)}, u32[]{:S(2)}) %collective-permute-start.4) | collective-permute-done | bytes 262176 | tf_op jit(solution)/shard_map/ppermute | solution.py:197
  59.2 9.4 %collective-permute-done.7 = bf16[256,1024]{1,0:T(8,128)(2,1)} collective-permute-done((bf16[256,1024]{1,0:T(8,128)(2,1)S(1)}, bf16[256,1024]{1,0:T(8,128)(2,1)}, u32[]{:S(2)}, u32[]{:S(2)}) %collective-permute-start.7) | collective-permute-done | bytes 524320 | tf_op jit(solution)/shard_map/ppermute | solution.py:197
  70.2 2.1 broadcast_select_fusion.5
  75.2 1.6 copy.222
  77.2 14.3 %attend.1 = (f32[64,2048]{1,0:T(8,128)S(1)}, f32[1,2048]{1,0:T(1,128)S(1)}) custom-call(s32[4,4]{1,0:T(4,128)S(1)} %pad_add_fusion.ranges, s32[1]{0:T(128)} %bitcast.5.flips, bf16[64,2048]{1,0:T(8,128)(2,1)S(1)} %copy_bitcast_fusion.2.q_ref, bf16[64,4096]{1,0:T(8,128)(2,1)S(1)} %squeeze.53.k_ref, bf16[64,4096]{1,0:T(8,128)(2,1)S(1)} %squeeze.54.v_ref, ...), custom_call_target="tpu_custom_call" | custom-call | tf_op jit(solution)/shard_map/attend/pallas_call | solution.py:86
  92.3 6.0 %all-to-all-start.1 = ((bf16[16,1,64,128]{3,2,1,0:T(8,128)(2,1)}), bf16[16,1,64,128]{3,2,1,0:T(8,128)(2,1)S(1)}, u32[]{:S(2)}, u32[]{:S(2)}) async-start(bf16[16,1,64,128]{3,2,1,0:T(8,128)(2,1)} %bitcast_bitcast_fusion), calls=%async_computation.1 | async-start | bytes 524288 | tf_op jit(solution)/shard_map/all_to_all | solution.py:318
  98.3 2.2 broadcast_select_fusion.1
  100.5 2.2 broadcast_select_fusion.3
  102.8 5.5 all-to-all-done.1
  111.7 1.6 convolution_add_fusion.7
  113.3 2.1 collective-permute-done.1
  117.6 2.0 fusion.26
  123.8 2.2 fusion.128
  126.0 2.2 convolution_add_fusion.5
  128.2 2.1 fusion.129
  130.3 2.3 fusion.130
  132.6 1.8 fusion.131
  138.7 4.9 collective-permute-done.9
  143.6 3.8 multiply_convert_fusion
  147.4 3.6 fusion.7
  155.9 5.7 collective-permute-done.12
  161.9 2.5 collective-permute-done.10
  171.4 1.6 fusion.20
  173.0 1.9 fusion.29
  174.9 1.8 fusion.133
  176.7 1.6 multiply_reduce_fusion.1
  182.0 3.0 collective-permute-done.13
  185.7 1.7 copy.233
  187.3 1.7 copy.234
  190.7 4.7 all-to-all-start.2
  197.5 4.3 convolution_convert_fusion
  201.7 3.7 all-to-all-done.2
  206.5 17.0 %attend_back.1 = (bf16[64,2048]{1,0:T(8,128)(2,1)S(1)}, f32[64,4096]{1,0:T(8,128)S(1)}, f32[64,4096]{1,0:T(8,128)S(1)}) custom-call(s32[4,4]{1,0:T(4,128)S(1)} %pad_add_fusion.ranges, s32[1]{0:T(128)} %bitcast.5.flips, bf16[64,2048]{1,0:T(8,128)(2,1)S(1)} %copy_bitcast_fusion.2.q_ref, bf16[64,4096]{1,0:T(8,128)(2,1)S(1)} %squeeze.53.k_ref, ...), custom_call_target="tpu_custom_call" | custom-call | tf_op jit(solution)/shard_map/attend_back/pallas_call | solution.py:160
  224.5 2.1 stack.89
  231.0 4.4 convolution_convert_fusion.1
  237.4 1.7 fusion.137
  240.5 3.7 all-to-all-start.3
  247.9 2.4 add_convert_fusion.1
  250.3 4.6 collective-permute-done.19
  256.3 2.4 add_convert_fusion
  258.7 4.2 all-to-all-done.3
  264.4 1.6 convolution_convert_fusion.2
  266.0 1.6 convolution_convert_fusion.3
  267.6 1.6 convolution_convert_fusion.4
  274.0 6.3 %collective-permute-done.17 = bf16[2,128,512]{1,2,0:T(8,128)(2,1)S(1)} collective-permute-done((bf16[2,128,512]{1,2,0:T(8,128)(2,1)S(1)}, bf16[2,128,512]{1,2,0:T(8,128)(2,1)S(1)}, u32[]{:S(2)}, u32[]{:S(2)}) %collective-permute-start.17) | collective-permute-done | bytes 262176 | tf_op jit(solution)/shard_map/ppermute | solution.py:197
  280.3 78.7 %all-reduce.5 = bf16[2,128,512]{1,2,0:T(8,128)(2,1)S(1)} all-reduce(f32[2,128,512]{1,2,0:T(8,128)S(1)} %maximum_add_fusion), channel_id=1, replica_groups=mesh['blk'=16,'tp'=2] {'blk'}, use_global_device_ids=true, to_apply=%region_28.29 | all-reduce | flops 131072 | bytes 786432 | tf_op jit(solution)/shard_map/psum | solution.py:462
  359.5 1.8 copy.242
  361.7 1.8 copy.243
  363.5 1.9 fusion.76
  365.9 1.7 collective-permute-start.18
  372.3 6.8 %collective-permute-done.15 = bf16[128,1024]{1,0:T(8,128)(2,1)S(1)} collective-permute-done((bf16[128,1024]{1,0:T(8,128)(2,1)S(1)}, bf16[128,1024]{1,0:T(8,128)(2,1)S(1)}, u32[]{:S(2)}, u32[]{:S(2)}) %collective-permute-start.15) | collective-permute-done | bytes 262176 | tf_op jit(solution)/shard_map/ppermute | solution.py:197
  381.2 38.8 %psum.71 = f32[6,1024]{1,0:T(8,128)S(1)} all-reduce(f32[6,1024]{1,0:T(8,128)S(1)} %stack.104), channel_id=1, replica_groups=mesh['blk'=16,'tp'=2] {'blk','tp'}, use_global_device_ids=true, to_apply=%region_35.36 | all-reduce | flops 6144 | bytes 49152 | tf_op jit(solution)/shard_map/psum | solution.py:472
  421.5 126.3 %all-reduce.4.cloned.1.call-done = (bf16[1024,512]{1,0:T(8,128)(2,1)}, bf16[1024,512]{1,0:T(8,128)(2,1)}, bf16[1024,512]{1,0:T(8,128)(2,1)}, bf16[512,1024]{1,0:...) async-done(((bf16[1024,512]{1,0:T(8,128)(2,1)}, bf16[1024,512]{1,0:T(8,128)(2,1)}, ...) | async-done | bytes 14680080 | tf_op jit(solution)/shard_map/psum | solution.py:477
  547.8 6.8 %convert_element_type.312 = f32[1024,2048]{1,0:T(8,128)} convert(bf16[1024,2048]{1,0:T(8,128)(2,1)} %get-tuple-element.146) | non-fusion elementwise | flops 2097152 | bytes 12582912 | tf_op jit(solution)/shard_map/convert_element_type | solution.py:477
  554.6 4.4 convert_element_type.314
  559.0 1.6 convert_element_type.300
  560.7 1.6 convert_element_type.302
  562.3 1.6 convert_element_type.304
  563.9 1.6 convert_element_type.306
  565.5 1.6 convert_element_type.308
  (363 shorter events, 90.2 us)
Async XLA Ops:
  7.2 25.0 %copy-start = (bf16[512,1024]{1,0:T(8,128)(2,1)S(1)}, bf16[512,1024]{1,0:T(8,128)(2,1)}, u32[]{:S(2)}) copy-start(bf16[512,1024]{1,0:T(8,128)(2,1)} %param.38) | copy-start | bytes 3145732
  14.8 10.2 %copy-start.12 = (bf16[512,1024]{1,0:T(8,128)(2,1)S(1)}, bf16[512,1024]{1,0:T(8,128)(2,1)}, u32[]{:S(2)}) copy-start(bf16[512,1024]{1,0:T(8,128)(2,1)} %param.34) | copy-start | bytes 3145732
  16.1 11.2 %copy-start.10 = (bf16[1024,512]{1,0:T(8,128)(2,1)S(1)}, bf16[1024,512]{1,0:T(8,128)(2,1)}, u32[]{:S(2)}) copy-start(bf16[1024,512]{1,0:T(8,128)(2,1)} %param.35) | copy-start | bytes 3145732
  17.2 11.5 %copy-start.15 = (bf16[128,1024]{1,0:T(8,128)(2,1)S(1)}, bf16[128,1024]{1,0:T(8,128)(2,1)}, u32[]{:S(2)}) copy-start(bf16[128,1024]{1,0:T(8,128)(2,1)} %param.23) | copy-start | bytes 786436
  17.2 51.4 %all-to-all-start = ((bf16[16,3,64,128]{3,2,1,0:T(8,128)(2,1)}), bf16[16,3,64,128]{3,2,1,0:T(8,128)(2,1)}, u32[]{:S(2)}, u32[]{:S(2)}) async-start(bf16[16,3,64,128]{3,2,1,0:T(8,128)(2,1)} %bitcast.251), calls=%async_computation | async-start | bytes 1572864 | tf_op jit(solution)/shard_map/all_to_all | solution.py:313
  25.8 15.0 %collective-permute-start.2 = (bf16[256,1024]{1,0:T(8,128)(2,1)}, bf16[256,1024]{1,0:T(8,128)(2,1)}, u32[]{:S(2)}, u32[]{:S(2)}) collective-permute-start(bf16[256,1024]{1,0:T(8,128)(2,1)} %constant_dynamic-slice_fusion.5), channel_id=1, source_target_pairs={{0,1},{1,0},{2,3},{3,2},{4,5},{5,4},{6,7},{7,6},{8,9},{9,8},{10,11... | collective-permute-start | bytes 1572872 | tf_op jit(solution)/shard_map/ppermute | solution.py:197
  28.2 6.0 %copy-start.90 = (s32[128]{0:T(128)S(1)}, s32[128]{0:T(128)}, u32[]{:S(2)}) copy-start(s32[128]{0:T(128)} %param.24) | copy-start | bytes 1540
  28.2 31.0 %collective-permute-start.5 = (bf16[512,512]{1,0:T(8,128)(2,1)}, bf16[512,512]{1,0:T(8,128)(2,1)}, u32[]{:S(2)}, u32[]{:S(2)}) collective-permute-start(bf16[512,512]{1,0:T(8,128)(2,1)} %constant_dynamic-slice_fusion.4), channel_id=1, source_target_pairs={{0,1},{1,0},{2,3},{3,2},{4,5},{5,4},{6,7},{7,6},{8,9},{9,8},{10,11... | collective-permute-start | bytes 1572872 | tf_op jit(solution)/shard_map/ppermute | solution.py:197
  30.6 27.0 %collective-permute-start.4 = (bf16[2,128,512]{2,1,0:T(8,128)(2,1)S(1)}, bf16[2,128,512]{2,1,0:T(8,128)(2,1)S(1)}, u32[]{:S(2)}, u32[]{:S(2)}) collective-permute-start(bf16[2,128,512]{2,1,0:T(8,128)(2,1)S(1)} %pad_maximum_fusion.20), channel_id=1, source_target_pairs={{0,1},{1,0},{2,3},{3,2},{4,5},{5,4},{6,7},{7,6},{8,9},{9,8},{10,11... | collective-permute-start | bytes 786440 | tf_op jit(solution)/shard_map/ppermute | solution.py:197
  32.2 36.4 %collective-permute-start.7 = (bf16[256,1024]{1,0:T(8,128)(2,1)S(1)}, bf16[256,1024]{1,0:T(8,128)(2,1)}, u32[]{:S(2)}, u32[]{:S(2)}) collective-permute-start(bf16[256,1024]{1,0:T(8,128)(2,1)S(1)} %constant_dynamic-slice_fusion.3), channel_id=1, source_target_pairs={{0,1},{1,0},{2,3},{3,2},{4,5},{5,4},{6,7},{7,6},{8,9},{9,8},{10,11... | collective-permute-start | bytes 1572872 | tf_op jit(solution)/shard_map/ppermute | solution.py:197
  40.9 29.4 %collective-permute-start.3 = (bf16[256,1024]{1,0:T(8,128)(2,1)}, bf16[256,1024]{1,0:T(8,128)(2,1)S(1)}, u32[]{:S(2)}, u32[]{:S(2)}) collective-permute-start(bf16[256,1024]{1,0:T(8,128)(2,1)} %collective-permute-done.2), channel_id=1, source_target_pairs={{0,2},{2,0},{4,6},{6,4},{8,10},{10,8},{12,14},{14,12},{16,18},{18,... | collective-permute-start | bytes 1572872 | tf_op jit(solution)/shard_map/ppermute | solution.py:201
  59.2 39.1 %collective-permute-start.6 = (bf16[512,512]{1,0:T(8,128)(2,1)}, bf16[512,512]{1,0:T(8,128)(2,1)}, u32[]{:S(2)}, u32[]{:S(2)}) collective-permute-start(bf16[512,512]{1,0:T(8,128)(2,1)} %collective-permute-done.5), channel_id=1, source_target_pairs={{0,2},{2,0},{4,6},{6,4},{8,10},{10,8},{12,14},{14,12},{16,18},{18,... | collective-permute-start | bytes 1572872 | tf_op jit(solution)/shard_map/ppermute | solution.py:201
  68.6 32.0 %collective-permute-start.8 = (bf16[256,1024]{1,0:T(8,128)(2,1)}, bf16[256,1024]{1,0:T(8,128)(2,1)}, u32[]{:S(2)}, u32[]{:S(2)}) collective-permute-start(bf16[256,1024]{1,0:T(8,128)(2,1)} %collective-permute-done.7), channel_id=1, source_target_pairs={{0,2},{2,0},{4,6},{6,4},{8,10},{10,8},{12,14},{14,12},{16,18},{18,... | collective-permute-start | bytes 1572872 | tf_op jit(solution)/shard_map/ppermute | solution.py:201
  69.7 3.6 collective-permute-start
  92.3 16.0 %all-to-all-start.1 = ((bf16[16,1,64,128]{3,2,1,0:T(8,128)(2,1)}), bf16[16,1,64,128]{3,2,1,0:T(8,128)(2,1)S(1)}, u32[]{:S(2)}, u32[]{:S(2)}) async-start(bf16[16,1,64,128]{3,2,1,0:T(8,128)(2,1)} %bitcast_bitcast_fusion), calls=%async_computation.1 | async-start | bytes 524288 | tf_op jit(solution)/shard_map/all_to_all | solution.py:318
  109.0 6.4 %copy-start.25 = (bf16[256,1024]{1,0:T(8,128)(2,1)S(1)}, bf16[256,1024]{1,0:T(8,128)(2,1)}, u32[]{:S(2)}) copy-start(bf16[256,1024]{1,0:T(8,128)(2,1)} %get-tuple-element.158) | copy-start | bytes 1572868
  109.0 6.4 %copy-start.27 = (bf16[256,1024]{1,0:T(8,128)(2,1)S(1)}, bf16[256,1024]{1,0:T(8,128)(2,1)}, u32[]{:S(2)}) copy-start(bf16[256,1024]{1,0:T(8,128)(2,1)} %get-tuple-element.159) | copy-start | bytes 1572868
  110.1 5.8 %copy-start.33 = (bf16[8,1,1,64,128]{4,3,1,0,2:T(8,128)(2,1)}, bf16[8,1,1,64,128]{4,3,1,0,2:T(8,128)(2,1)S(1)}, u32[]{:S(2)}) copy-start(bf16[8,1,1,64,128]{4,3,1,0,2:T(8,128)(2,1)S(1)} %get-tuple-element.177) | copy-start | bytes 393220
  110.1 5.8 %copy-start.61 = (bf16[8,1,1,64,128]{4,3,1,0,2:T(8,128)(2,1)}, bf16[8,1,1,64,128]{4,3,1,0,2:T(8,128)(2,1)S(1)}, u32[]{:S(2)}) copy-start(bf16[8,1,1,64,128]{4,3,1,0,2:T(8,128)(2,1)S(1)} %get-tuple-element.176) | copy-start | bytes 393220
  110.1 5.3 collective-permute-start.1
  111.7 5.0 copy-start.86
  111.7 5.0 copy-start.88
  117.6 5.0 copy-start.75
  122.6 5.6 copy-start.69
  126.0 6.6 %copy-start.67 = (bf16[128,8,64]{0,2,1:T(8,128)(2,1)}, bf16[128,8,64]{0,2,1:T(8,128)(2,1)S(1)}, u32[]{:S(2)}) copy-start(bf16[128,8,64]{0,2,1:T(8,128)(2,1)S(1)} %get-tuple-element.192) | copy-start | bytes 393220
  136.1 7.5 %collective-permute-start.9 = (bf16[128,1024]{1,0:T(8,128)(2,1)}, bf16[128,1024]{1,0:T(8,128)(2,1)}, u32[]{:S(2)}, u32[]{:S(2)}) collective-permute-start(bf16[128,1024]{1,0:T(8,128)(2,1)} %add_convert_fusion.3), channel_id=1, source_target_pairs={{0,1},{1,0},{2,3},{3,2},{4,5},{5,4},{6,7},{7,6},{8,9},{9,8},{10,11... | collective-permute-start | bytes 786440 | tf_op jit(solution)/shard_map/ppermute | solution.py:197
  138.6 8.8 %copy-start.45 = (bf16[128,1024]{1,0:T(8,128)(2,1)}, bf16[128,1024]{1,0:T(8,128)(2,1)S(1)}, u32[]{:S(2)}) copy-start(bf16[128,1024]{1,0:T(8,128)(2,1)S(1)} %get-tuple-element.169) | copy-start | bytes 786436
  138.7 8.8 %copy-start.92 = (bf16[2048,1024]{1,0:T(8,128)(2,1)S(1)}, bf16[2048,1024]{1,0:T(8,128)(2,1)}, u32[]{:S(2)}) copy-start(bf16[2048,1024]{1,0:T(8,128)(2,1)} %param.40) | copy-start | bytes 12582916
  147.4 6.6 %copy-start.19 = (bf16[256,2048]{1,0:T(8,128)(2,1)}, bf16[256,2048]{1,0:T(8,128)(2,1)S(1)}, u32[]{:S(2)}) copy-start(bf16[256,2048]{1,0:T(8,128)(2,1)S(1)} %get-tuple-element.200) | copy-start | bytes 3145732
  152.4 9.2 %collective-permute-start.12 = (bf16[128,1024]{1,0:T(8,128)(2,1)S(1)}, bf16[128,1024]{1,0:T(8,128)(2,1)S(1)}, u32[]{:S(2)}, u32[]{:S(2)}) collective-permute-start(bf16[128,1024]{1,0:T(8,128)(2,1)S(1)} %slice.110), channel_id=1, source_target_pairs={{0,1},{1,0},{2,3},{3,2},{4,5},{5,4},{6,7},{7,6},{8,9},{9,8},{10,11... | collective-permute-start | bytes 786440 | tf_op jit(solution)/shard_map/ppermute | solution.py:197
  154.0 7.6 %copy-start.6 = (f32[128,1024]{1,0:T(8,128)S(1)}, f32[128,1024]{1,0:T(8,128)}, u32[]{:S(2)}) copy-start(f32[128,1024]{1,0:T(8,128)} %copy-done.5) | copy-start | bytes 1572868
  155.3 9.1 %collective-permute-start.10 = (bf16[128,1024]{1,0:T(8,128)(2,1)S(1)}, bf16[128,1024]{1,0:T(8,128)(2,1)S(1)}, u32[]{:S(2)}, u32[]{:S(2)}) collective-permute-start(bf16[128,1024]{1,0:T(8,128)(2,1)S(1)} %slice.154), channel_id=1, source_target_pairs={{0,1},{1,0},{2,3},{3,2},{4,5},{5,4},{6,7},{7,6},{8,9},{9,8},{10,11... | collective-permute-start | bytes 786440 | tf_op jit(solution)/shard_map/ppermute | solution.py:197
  168.0 5.0 copy-start.71
  170.4 6.3 %copy-start.49 = (bf16[8,128,128]{2,1,0:T(8,128)(2,1)}, bf16[8,128,128]{2,1,0:T(8,128)(2,1)S(1)}, u32[]{:S(2)}) copy-start(bf16[8,128,128]{2,1,0:T(8,128)(2,1)S(1)} %fusion.21) | copy-start | bytes 786436
  170.6 6.0 %copy-start.35 = (bf16[8,64,128]{2,1,0:T(8,128)(2,1)}, bf16[8,64,128]{2,1,0:T(8,128)(2,1)S(1)}, u32[]{:S(2)}) copy-start(bf16[8,64,128]{2,1,0:T(8,128)(2,1)S(1)} %fusion.28) | copy-start | bytes 393220
  171.4 5.3 copy-start.4
  171.4 5.3 copy-start.64
  171.4 5.3 copy-start.66
  179.4 6.3 %copy-start.23 = (bf16[128,1024]{1,0:T(8,128)(2,1)}, bf16[128,1024]{1,0:T(8,128)(2,1)S(1)}, u32[]{:S(2)}) copy-start(bf16[128,1024]{1,0:T(8,128)(2,1)S(1)} %get-tuple-element.148) | copy-start | bytes 786436
  179.9 17.6 %copy-start.20 = (bf16[256,2048]{1,0:T(8,128)(2,1)S(1)}, bf16[256,2048]{1,0:T(8,128)(2,1)}, u32[]{:S(2)}) copy-start(bf16[256,2048]{1,0:T(8,128)(2,1)} %copy-done.19) | copy-start | bytes 3145732
  179.9 5.0 collective-permute-start.13
  190.7 14.7 %all-to-all-start.2 = ((bf16[16,1,64,128]{3,2,1,0:T(8,128)(2,1)}), bf16[16,1,64,128]{3,2,1,0:T(8,128)(2,1)}, u32[]{:S(2)}, u32[]{:S(2)}) async-start(bf16[16,1,64,128]{3,2,1,0:T(8,128)(2,1)} %bitcast.264), calls=%async_computation.2 | async-start | bytes 524288 | tf_op jit(solution)/shard_map/all_to_all | solution.py:422
  195.4 60.9 %collective-permute-start.22 = (bf16[128,512]{0,1:T(8,128)(2,1)}, bf16[128,512]{0,1:T(8,128)(2,1)}, u32[]{:S(2)}, u32[]{:S(2)}) collective-permute-start(bf16[128,512]{0,1:T(8,128)(2,1)} %bitcast.299), channel_id=1, source_target_pairs={{0,1},{1,0},{2,3},{3,2},{4,5},{5,4},{6,7},{7,6},{8,9},{9,8},{10,11... | collective-permute-start | bytes 393224 | tf_op jit(solution)/shard_map/ppermute | solution.py:197
  197.0 51.0 %collective-permute-start.20 = (bf16[128,1024]{1,0:T(8,128)(2,1)}, bf16[128,1024]{1,0:T(8,128)(2,1)}, u32[]{:S(2)}, u32[]{:S(2)}) collective-permute-start(bf16[128,1024]{1,0:T(8,128)(2,1)} %add_convert_fusion.4), channel_id=1, source_target_pairs={{0,1},{1,0},{2,3},{3,2},{4,5},{5,4},{6,7},{7,6},{8,9},{9,8},{10,11... | collective-permute-start | bytes 786440 | tf_op jit(solution)/shard_map/ppermute | solution.py:197
  230.9 6.5 %copy-start.68 = (bf16[128,8,64]{0,2,1:T(8,128)(2,1)S(1)}, bf16[128,8,64]{0,2,1:T(8,128)(2,1)}, u32[]{:S(2)}) copy-start(bf16[128,8,64]{0,2,1:T(8,128)(2,1)} %copy-done.67) | copy-start | bytes 393220
  230.9 8.3 %collective-permute-start.14 = (bf16[2,64,16,1,128]{4,2,1,0,3:T(8,128)(2,1)S(1)}, bf16[2,64,16,1,128]{4,2,1,0,3:T(8,128)(2,1)S(1)}, u32[]{:S(2)}, u32[]{:S(2)}) collective-permute-start(bf16[2,64,16,1,128]{4,2,1,0,3:T(8,128)(2,1)S(1)} %fusion.50), channel_id=1, source_target_pairs={{0,2},{2,0},{4,6},{6,4},{8,10},{10,8},{12,14},{14,12},{16,18},{18,... | collective-permute-start | bytes 1572872 | tf_op jit(solution)/shard_map/ppermute | solution.py:201
  235.4 20.9 %collective-permute-start.23 = (bf16[128,1024]{1,0:T(8,128)(2,1)S(1)}, bf16[128,1024]{1,0:T(8,128)(2,1)}, u32[]{:S(2)}, u32[]{:S(2)}) collective-permute-start(bf16[128,1024]{1,0:T(8,128)(2,1)S(1)} %copy-done.22), channel_id=1, source_target_pairs={{0,1},{1,0},{2,3},{3,2},{4,5},{5,4},{6,7},{7,6},{8,9},{9,8},{10,11... | collective-permute-start | bytes 786440 | tf_op jit(solution)/shard_map/ppermute | solution.py:197
  236.9 11.0 %collective-permute-start.21 = (bf16[128,512]{0,1:T(8,128)(2,1)}, bf16[128,512]{0,1:T(8,128)(2,1)S(1)}, u32[]{:S(2)}, u32[]{:S(2)}) collective-permute-start(bf16[128,512]{0,1:T(8,128)(2,1)} %bitcast.41), channel_id=1, source_target_pairs={{0,1},{1,0},{2,3},{3,2},{4,5},{5,4},{6,7},{7,6},{8,9},{9,8},{10,11... | collective-permute-start | bytes 393224 | tf_op jit(solution)/shard_map/ppermute | solution.py:197
  239.3 5.2 copy-start.36
  240.5 5.4 copy-start.24
  240.5 5.4 copy-start.34
  240.5 22.4 %all-to-all-start.3 = ((bf16[16,3,64,128]{3,2,1,0:T(8,128)(2,1)}), bf16[16,3,64,128]{3,2,1,0:T(8,128)(2,1)S(1)}, u32[]{:S(2)}, u32[]{:S(2)}) async-start(bf16[16,3,64,128]{3,2,1,0:T(8,128)(2,1)} %copy.240), calls=%async_computation.3 | async-start | bytes 1572864 | tf_op jit(solution)/shard_map/all_to_all | solution.py:318
  244.3 303.5 %all-reduce.4.cloned.1.call-start = ((), (), s32[]{:S(2)}) async-start(), calls=%async_computation.4 | async-start | bytes 29360128 | tf_op jit(solution)/shard_map/psum | solution.py:477
  246.3 8.6 %copy-start.62 = (bf16[8,1,1,64,128]{4,3,1,0,2:T(8,128)(2,1)S(1)}, bf16[8,1,1,64,128]{4,3,1,0,2:T(8,128)(2,1)}, u32[]{:S(2)}) copy-start(bf16[8,1,1,64,128]{4,3,1,0,2:T(8,128)(2,1)} %copy-done.61) | copy-start | bytes 393220
  246.4 8.6 %collective-permute-start.19 = (bf16[128,1024]{1,0:T(8,128)(2,1)S(1)}, bf16[128,1024]{1,0:T(8,128)(2,1)S(1)}, u32[]{:S(2)}, u32[]{:S(2)}) collective-permute-start(bf16[128,1024]{1,0:T(8,128)(2,1)S(1)} %copy-done.24), channel_id=1, source_target_pairs={{0,1},{1,0},{2,3},{3,2},{4,5},{5,4},{6,7},{7,6},{8,9},{9,8},{10,11... | collective-permute-start | bytes 786440 | tf_op jit(solution)/shard_map/ppermute | solution.py:197
  250.3 6.0 %copy-start.9 = (f32[512,1024]{1,0:T(8,128)S(1)}, f32[512,1024]{1,0:T(8,128)}, u32[]{:S(2)}) copy-start(f32[512,1024]{1,0:T(8,128)} %fusion.137) | copy-start | bytes 6291460
  258.7 5.6 copy-start.8
  271.0 9.2 %collective-permute-start.17 = (bf16[2,128,512]{1,2,0:T(8,128)(2,1)S(1)}, bf16[2,128,512]{1,2,0:T(8,128)(2,1)S(1)}, u32[]{:S(2)}, u32[]{:S(2)}) collective-permute-start(bf16[2,128,512]{1,2,0:T(8,128)(2,1)S(1)} %pad_maximum_fusion.22), channel_id=1, source_target_pairs={{0,1},{1,0},{2,3},{3,2},{4,5},{5,4},{6,7},{7,6},{8,9},{9,8},{10,11... | collective-permute-start | bytes 786440 | tf_op jit(solution)/shard_map/ppermute | solution.py:197
  273.1 97.3 %collective-permute-start.11 = (bf16[128,1024]{1,0:T(8,128)(2,1)}, bf16[128,1024]{1,0:T(8,128)(2,1)}, u32[]{:S(2)}, u32[]{:S(2)}) collective-permute-start(bf16[128,1024]{1,0:T(8,128)(2,1)} %get-tuple-element.167), channel_id=1, source_target_pairs={{0,1},{1,0},{2,3},{3,2},{4,5},{5,4},{6,7},{7,6},{8,9},{9,8},{10,11... | collective-permute-start | bytes 786440 | tf_op jit(solution)/shard_map/ppermute | solution.py:197
  365.9 14.4 %collective-permute-start.18 = (bf16[128,1024]{1,0:T(8,128)(2,1)S(1)}, bf16[128,1024]{1,0:T(8,128)(2,1)S(1)}, u32[]{:S(2)}, u32[]{:S(2)}) collective-permute-start(bf16[128,1024]{1,0:T(8,128)(2,1)S(1)} %fusion.22), channel_id=1, source_target_pairs={{0,1},{1,0},{2,3},{3,2},{4,5},{5,4},{6,7},{7,6},{8,9},{9,8},{10,11... | collective-permute-start | bytes 786440 | tf_op jit(solution)/shard_map/ppermute | solution.py:197
  370.0 9.5 %copy-start.31 = (f32[128,1024]{1,0:T(8,128)S(1)}, f32[128,1024]{1,0:T(8,128)}, u32[]{:S(2)}) copy-start(f32[128,1024]{1,0:T(8,128)} %get-tuple-element.149) | copy-start | bytes 1572868
  370.0 9.1 %collective-permute-start.15 = (bf16[128,1024]{1,0:T(8,128)(2,1)S(1)}, bf16[128,1024]{1,0:T(8,128)(2,1)S(1)}, u32[]{:S(2)}, u32[]{:S(2)}) collective-permute-start(bf16[128,1024]{1,0:T(8,128)(2,1)S(1)} %constant_dynamic-slice_fusion), channel_id=1, source_target_pairs={{0,1},{1,0},{2,3},{3,2},{4,5},{5,4},{6,7},{7,6},{8,9},{9,8},{10,11... | collective-permute-start | bytes 786440 | tf_op jit(solution)/shard_map/ppermute | solution.py:197
  379.8 40.8 %collective-permute-start.16 = (bf16[128,1024]{1,0:T(8,128)(2,1)S(1)}, bf16[128,1024]{1,0:T(8,128)(2,1)S(1)}, u32[]{:S(2)}, u32[]{:S(2)}) collective-permute-start(bf16[128,1024]{1,0:T(8,128)(2,1)S(1)} %fusion.46), channel_id=1, source_target_pairs={{0,1},{1,0},{2,3},{3,2},{4,5},{5,4},{6,7},{7,6},{8,9},{9,8},{10,11... | collective-permute-start | bytes 786440 | tf_op jit(solution)/shard_map/ppermute | solution.py:197
  547.8 6.8 %copy-start.14 = (bf16[2048,1024]{1,0:T(8,128)(2,1)S(1)}, bf16[2048,1024]{1,0:T(8,128)(2,1)}, u32[]{:S(2)}) copy-start(bf16[2048,1024]{1,0:T(8,128)(2,1)} %get-tuple-element.147) | copy-start | bytes 12582916
  (60 other events, 158.4 us)
Sparse Core Ops, SparseCore 0:
  269.3 278.4 all-reduce.3
